TPU v7x, 768 devices: a whole 4x8x12 slice. The times are simulated.
768 devices in a mesh: lat: 64 (over y, x, core), lon: 12 (over z).
Axes of the slice: x: 4, y: 8, z: 12, core: 2. Of those that a mesh axis runs over, the one named last changes fastest.
Arguments:
- control: float32 [1024, 32, 1536], P('lat', None, 'lon'), may hold values from -6 to 6
- background: float32 [1024, 32, 1536], P('lat', None, 'lon'), may hold values from -6 to 6
- lon_width: int32 [1024], P('lat'), may hold values from 2 to 16
- block_cells: int32 [4096, 12], P('lat', 'lon'), may hold values from 0 to 255, as said below
- block_owner: int32 [4096, 12], P('lat', 'lon'), may hold values from -1 to 63, as said below
- channel_count: int32 [2112, 12], P('lat', 'lon'), may hold values from 1 to 256
- radiance: bfloat16 [16384, 3168], P('lat', 'lon'), may hold values from -6 to 6
- in_weight: bfloat16 [32, 1024], replicated, may hold values from -1 to 1
- in_bias: float32 [1024], replicated, may hold values from -3 to 3
- mid_weight: bfloat16 [1024, 1024], replicated, may hold values from -0.1875 to 0.1875
- mid_bias: float32 [1024], replicated, may hold values from -3 to 3
- out_weight: bfloat16 [1024, 256], replicated, may hold values from -0.1875 to 0.1875
- out_bias: float32 [256], replicated, may hold values from -3 to 3
Outputs:
- gradient: float32 [1024, 32, 1536], P('lat', None, 'lon')
Inputs may be any that keep to these rules, and one draw needn't show every extreme that they name: `block_owner`: the live slots of a device come first, unused ones hold -1. Every device has at least 16 observed blocks, some device of every lon index has 64. One device sends at most 1 block to one owner, and an owner receives at most 33 blocks from its lon index; both bounds are reached in every draw. `block_cells`: the live slots of one device name distinct blocks.
All inputs are finite; a program needn't handle non-finite values.
Results may differ from a plain program's by a relative error of at most 0.0023.
Values may be sent and summed in bfloat16 or wider, within the bound.
A program may use at most 32 MiB of HBM per device.

v0:
```python
import jax
import jax.numpy as jnp
from jax import lax
from jax.sharding import PartitionSpec as P

REACH = 16
BLOCK_COLS = 8


lat_sigma = 8.0


def padded_2(block, sides, width, periodic):
    for axis, dim in sides:
        count = lax.axis_size(axis)
        forward = [(i, i + 1) for i in range(count - 1)]
        if periodic:
            forward.append((count - 1, 0))
        backward = [(target, source) for source, target in forward]
        low = lax.ppermute(
            lax.slice_in_dim(block, block.shape[dim] - width, None, axis=dim), axis, forward
        )
        high = lax.ppermute(lax.slice_in_dim(block, 0, width, axis=dim), axis, backward)
        block = jnp.concatenate([low, block, high], axis=dim)
    return block


def lat_band(height, span):
    out_ids = lax.broadcasted_iota(jnp.int32, (height, span), 0)
    in_ids = lax.broadcasted_iota(jnp.int32, (height, span), 1)
    offsets = (in_ids - out_ids - REACH).astype(jnp.float32)
    steps_all = jnp.arange(-REACH, REACH + 1).astype(jnp.float32)
    norm_scale = jnp.sqrt(jnp.sum(jnp.exp(-steps_all * steps_all / (lat_sigma * lat_sigma))))
    raw_taps = jnp.exp(-offsets * offsets / (2.0 * lat_sigma * lat_sigma)) / norm_scale
    return jnp.where(jnp.abs(offsets) <= REACH, raw_taps, 0.0)


def smooth_lat(padded, height):
    band_matrix = lat_band(height, padded.shape[0])
    return jnp.einsum("rq,qlc->rlc", band_matrix, padded, precision=lax.Precision.HIGHEST)


def lon_band(widths, span, width_out):
    spread = jnp.maximum(widths, 1).astype(jnp.float32)[:, None, None]
    in_ids = lax.broadcasted_iota(jnp.int32, (1, span, width_out), 1)
    out_ids = lax.broadcasted_iota(jnp.int32, (1, span, width_out), 2)
    offsets = (in_ids - out_ids - REACH).astype(jnp.float32)
    steps_all = jnp.arange(-REACH, REACH + 1).astype(jnp.float32)[None, :]
    row_spread = spread[:, :, 0]
    norm_scale = jnp.sqrt(
        jnp.sum(jnp.exp(-steps_all * steps_all / (row_spread * row_spread)), axis=1)
    )
    raw_taps = jnp.exp(-offsets * offsets / (2.0 * spread * spread)) / norm_scale[:, None, None]
    return jnp.where(jnp.abs(offsets) <= REACH, raw_taps, 0.0)


def smooth_lon(padded, widths):
    band_matrix = lon_band(widths, padded.shape[2], padded.shape[2] - 2 * REACH)
    return jnp.einsum("rlq,rqc->rlc", padded, band_matrix, precision=lax.Precision.HIGHEST)


def lat_rims(values):
    return padded_2(values, (("lat", 0),), REACH, False)


def lon_rims(values):
    return padded_2(values, (("lon", 2),), REACH, True)


def radiate(
    inputs, observed, kept_mask, in_weight, in_bias, mid_weight, mid_bias, out_weight, out_bias
):
    first_pre = (
        jnp.einsum("lh,lm->hm", in_weight, inputs, preferred_element_type=jnp.float32)
        + in_bias[:, None]
    )
    act_one = jnp.tanh(first_pre).astype(jnp.bfloat16)
    second_pre = (
        jnp.einsum("hk,hm->km", mid_weight, act_one, preferred_element_type=jnp.float32)
        + mid_bias[:, None]
    )
    act_two = jnp.tanh(second_pre).astype(jnp.bfloat16)
    emitted = (
        jnp.einsum("kn,km->nm", out_weight, act_two, preferred_element_type=jnp.float32)
        + out_bias[:, None]
    )
    misfit = jnp.where(kept_mask, emitted - observed.astype(jnp.float32), 0.0).astype(jnp.bfloat16)
    back_two = jnp.einsum("kn,nm->km", out_weight, misfit, preferred_element_type=jnp.float32)
    two_val = act_two.astype(jnp.float32)
    grad_two = (back_two * (1.0 - two_val * two_val)).astype(jnp.bfloat16)
    back_one = jnp.einsum("hk,km->hm", mid_weight, grad_two, preferred_element_type=jnp.float32)
    one_val = act_one.astype(jnp.float32)
    grad_one = (back_one * (1.0 - one_val * one_val)).astype(jnp.bfloat16)
    return jnp.einsum("lh,hm->lm", in_weight, grad_one, preferred_element_type=jnp.float32).astype(
        jnp.bfloat16
    )


def observe(
    profile,
    block_cells,
    block_owner,
    channel_count,
    radiance,
    in_weight,
    in_bias,
    mid_weight,
    mid_bias,
    out_weight,
    out_bias,
    lat_count,
):
    height = profile.shape[0]
    levels = profile.shape[1]
    width_cols = profile.shape[2]
    groups = width_cols // BLOCK_COLS
    cell_count = height * groups
    block_size = levels * BLOCK_COLS
    cells = jnp.transpose(
        profile.reshape(height, levels, groups, BLOCK_COLS), (0, 2, 1, 3)
    ).reshape(cell_count, block_size)
    owners = block_owner[:, 0]
    picked = block_cells[:, 0]
    slot_count = owners.shape[0]
    send_cap = (slot_count + lat_count - 1) // lat_count
    slot_ids = lax.broadcasted_iota(jnp.int32, (slot_count, slot_count), 1)
    here_ids = lax.broadcasted_iota(jnp.int32, (slot_count, slot_count), 0)
    arrival = jnp.sum(
        ((owners[None, :] == owners[:, None]) & (slot_ids < here_ids)).astype(jnp.int32), axis=1
    )
    dest_ids = lax.broadcasted_iota(jnp.int32, (lat_count, send_cap, slot_count), 0)
    rank_ids = lax.broadcasted_iota(jnp.int32, (lat_count, send_cap, slot_count), 1)
    select = ((owners[None, None, :] == dest_ids) & (arrival[None, None, :] == rank_ids)).astype(
        jnp.float32
    )
    cell_match = (
        picked[:, None] == lax.broadcasted_iota(jnp.int32, (slot_count, cell_count), 1)
    ).astype(jnp.float32)
    routing = jnp.einsum("oks,sr->okr", select, cell_match).astype(jnp.bfloat16)
    outgoing = jnp.einsum("okr,re->oke", routing, cells, preferred_element_type=jnp.float32).astype(
        jnp.bfloat16
    )
    slot_flags = jnp.sum(select, axis=2).astype(jnp.bfloat16)
    arrived, arrived_flags = (
        lax.all_to_all(outgoing, "lat", split_axis=0, concat_axis=0, tiled=True),
        lax.all_to_all(slot_flags, "lat", split_axis=0, concat_axis=0, tiled=True),
    )
    recv_most = channel_count.shape[0]
    present = (arrived_flags.reshape(-1) > 0.5).astype(jnp.int32)
    position = jnp.cumsum(present) - present
    recv_ids = lax.broadcasted_iota(jnp.int32, (recv_most, present.shape[0]), 0)
    compact = ((present[None, :] == 1) & (position[None, :] == recv_ids)).astype(jnp.bfloat16)
    blocks = jnp.einsum(
        "mf,fe->me", compact, arrived.reshape(-1, block_size), preferred_element_type=jnp.float32
    ).astype(jnp.bfloat16)
    inputs = jnp.transpose(blocks.reshape(recv_most, levels, BLOCK_COLS), (1, 0, 2)).reshape(
        levels, recv_most * BLOCK_COLS
    )
    filled = lax.broadcasted_iota(jnp.int32, (recv_most,), 0) < jnp.sum(present)
    col_counts = jnp.broadcast_to(channel_count[:, 0][:, None], (recv_most, BLOCK_COLS)).reshape(-1)
    col_filled = jnp.broadcast_to(filled[:, None], (recv_most, BLOCK_COLS)).reshape(-1)
    channel_ids = lax.broadcasted_iota(jnp.int32, (radiance.shape[0], 1), 0)
    kept_mask = (channel_ids < col_counts[None, :]) & col_filled[None, :]
    sensitivity = radiate(
        inputs, radiance, kept_mask, in_weight, in_bias, mid_weight, mid_bias, out_weight, out_bias
    )
    sens_blocks = jnp.transpose(
        sensitivity.reshape(levels, recv_most, BLOCK_COLS), (1, 0, 2)
    ).reshape(recv_most, block_size)
    returning = jnp.einsum(
        "mf,me->fe", compact, sens_blocks, preferred_element_type=jnp.float32
    ).astype(jnp.bfloat16)
    returned = lax.all_to_all(
        returning.reshape(lat_count, send_cap, block_size),
        "lat",
        split_axis=0,
        concat_axis=0,
        tiled=True,
    )
    landed = jnp.einsum("okr,oke->re", routing, returned, preferred_element_type=jnp.float32)
    return jnp.transpose(landed.reshape(height, groups, levels, BLOCK_COLS), (0, 2, 1, 3)).reshape(
        height, levels, width_cols
    )


def shards(
    control,
    background,
    lon_width,
    block_cells,
    block_owner,
    channel_count,
    radiance,
    in_weight,
    in_bias,
    mid_weight,
    mid_bias,
    out_weight,
    out_bias,
):
    height = control.shape[0]
    lat_count = lax.axis_size("lat")
    increment = smooth_lon(lon_rims(smooth_lat(lat_rims(control), height)), lon_width)
    profile = (background + increment).astype(jnp.bfloat16)
    landing = observe(
        profile,
        block_cells,
        block_owner,
        channel_count,
        radiance,
        in_weight,
        in_bias,
        mid_weight,
        mid_bias,
        out_weight,
        out_bias,
        lat_count,
    )
    adjoint = smooth_lat(lat_rims(smooth_lon(lon_rims(landing), lon_width)), height)
    return control + adjoint


def solution(mesh):
    return jax.shard_map(
        shards,
        mesh=mesh,
        in_specs=(
            P("lat", None, "lon"),
            P("lat", None, "lon"),
            P("lat"),
            P("lat", "lon"),
            P("lat", "lon"),
            P("lat", "lon"),
            P("lat", "lon"),
            P(),
            P(),
            P(),
            P(),
            P(),
            P(),
        ),
        out_specs=P("lat", None, "lon"),
        check_vma=False,
    )
```

profile of v0, /device:TPU:8, one launch (start us, length us, event | category | flops | bytes accessed | tf_op | source)
XLA Modules:
  0.0 132.9 jit_solution(11375522358873686860)
XLA Ops:
  1.3 1.9 %collective-permute-start = (f32[16,32,128]{2,0,1:T(8,128)S(1)}, f32[16,32,128]{2,0,1:T(8,128)S(1)}, u32[]{:S(2)}, u32[]{:S(2)}) collective-permute-start(f32[16,32,128]{2,0,1:T(8,128)S(1)} %copy.115), channel_id=1, source_target_pairs={{0,12},{12,24},{24,36},{36,48},{48,60},{60,72},{72,84},{84,96},{96... | collective-permute-start | bytes 786440 | tf_op jit(solution)/shard_map/ppermute | solution.py:20
  3.2 5.8 %collective-permute-start.1 = (f32[16,32,128]{2,0,1:T(8,128)S(1)}, f32[16,32,128]{2,0,1:T(8,128)S(1)}, u32[]{:S(2)}, u32[]{:S(2)}) collective-permute-start(f32[16,32,128]{2,0,1:T(8,128)S(1)} %copy.115), channel_id=1, source_target_pairs={{12,0},{24,12},{36,24},{48,36},{60,48},{72,60},{84,72},{96,84},{10... | collective-permute-start | bytes 786440 | tf_op jit(solution)/shard_map/ppermute | solution.py:23
  11.4 9.3 %all-to-all-start = ((bf16[64,1,1]{2,1,0:T(2,128)(2,1)}), bf16[64,1,1]{2,1,0:T(2,128)(2,1)S(1)}, u32[]{:S(2)}, u32[]{:S(2)}) async-start(bf16[64,1,1]{2,1,0:T(2,128)(2,1)} %copy.94), calls=%async_computation | async-start | bytes 65536 | tf_op jit(solution)/shard_map/all_to_all | solution.py:146
  26.3 3.0 %all-to-all-done = bf16[64,1,1]{2,1,0:T(2,128)(2,1)S(1)} async-done(((bf16[64,1,1]{2,1,0:T(2,128)(2,1)}), bf16[64,1,1]{2,1,0:T(2,128)(2,1)S(1)}, u32[]{:S(2)}, u32[]{:S(2)}) %all-to-all-start) | async-done | bytes 160 | tf_op jit(solution)/shard_map/all_to_all | solution.py:146
  29.3 1.8 %fusion.98 = (s32[]{:T(128)}, s32[64]{0:T(128)S(1)}) fusion(bf16[64,1,1]{2,1,0:T(2,128)(2,1)S(1)} %all-to-all-done), kind=kLoop, calls=%fused_computation.129 | loop fusion | flops 191 | bytes 388 | tf_op jit(solution)/shard_map/reduce_sum | solution.py:159
  31.9 4.3 %collective-permute-start.2 = (f32[16,32,16]{2,0,1:T(8,128)S(1)}, f32[16,32,16]{2,0,1:T(8,128)S(1)}, u32[]{:S(2)}, u32[]{:S(2)}) collective-permute-start(f32[16,32,16]{2,0,1:T(8,128)S(1)} %get-tuple-element.9), channel_id=1, source_target_pairs={{0,1},{1,2},{2,3},{3,4},{4,5},{5,6},{6,7},{7,8},{8,9},{9,10},{10,1... | collective-permute-start | bytes 98312 | tf_op jit(solution)/shard_map/ppermute | solution.py:20
  36.2 12.2 %collective-permute-start.3 = (f32[16,32,16]{2,0,1:T(8,128)S(1)}, f32[16,32,16]{2,0,1:T(8,128)S(1)}, u32[]{:S(2)}, u32[]{:S(2)}) collective-permute-start(f32[16,32,16]{2,0,1:T(8,128)S(1)} %get-tuple-element.10), channel_id=1, source_target_pairs={{1,0},{2,1},{3,2},{4,3},{5,4},{6,5},{7,6},{8,7},{9,8},{10,9},{11,1... | collective-permute-start | bytes 98312 | tf_op jit(solution)/shard_map/ppermute | solution.py:23
  49.9 2.9 %collective-permute-done.2 = f32[16,32,16]{2,0,1:T(8,128)S(1)} collective-permute-done((f32[16,32,16]{2,0,1:T(8,128)S(1)}, f32[16,32,16]{2,0,1:T(8,128)S(1)}, u32[]{:S(2)}, u32[]{:S(2)}) %collective-permute-start.2) | collective-permute-done | bytes 32800 | tf_op jit(solution)/shard_map/ppermute | solution.py:20
  54.3 2.3 %fusion.13 = bf16[16,32,128]{2,1,0:T(8,128)(2,1)S(1)} fusion(f32[16,32,128]{2,1,0:T(8,128)S(1)} %copy-done.5, f32[16]{0:T(128)} %sqrt.13, f32[16]{0:T(128)} %get-tuple-element.11, f32[160,128]{1,0:T(8,128)S(1)} %copy-done.2, pred[160,128]{1,0:T(8,128)(4,1)S(1)} %abs_compare_fusion, f32[16,32,160]{2,0,1:T(8,128)S(1)} %pad_maximum_fusion.1), kind=kOutput, calls=%fused_computation.22 | convolution fusion | flops 126943232 | bytes 823424 | tf_op jit(solution)/shard_map/rlq,rqc->rlc/dot_general | solution.py:59
  57.6 2.9 %copy.101 = bf16[16,16,32,8]{1,0,3,2:T(8,128)(2,1)S(1)} copy(bf16[16,16,32,8]{2,3,1,0:T(8,128)(2,1)} %bitcast.81) | data formatting | bytes 262144 | tf_op jit(solution)/shard_map/transpose | solution.py:119
  63.5 7.6 %all-to-all-start.1 = ((bf16[64,2,128]{2,1,0:T(2,128)(2,1)}), bf16[64,2,128]{2,1,0:T(2,128)(2,1)S(1)}, u32[]{:S(2)}, u32[]{:S(2)}) async-start(bf16[64,2,128]{2,1,0:T(2,128)(2,1)} %reshape.260), calls=%async_computation.1 | async-start | bytes 65536 | tf_op jit(solution)/shard_map/all_to_all | solution.py:145
  72.0 7.7 %all-to-all-done.1 = bf16[64,2,128]{2,1,0:T(2,128)(2,1)S(1)} async-done(((bf16[64,2,128]{2,1,0:T(2,128)(2,1)}), bf16[64,2,128]{2,1,0:T(2,128)(2,1)S(1)}, u32[]{:S(2)}, u32[]{:S(2)}) %all-to-all-start.1) | async-done | bytes 32800 | tf_op jit(solution)/shard_map/all_to_all | solution.py:145
  80.5 1.5 %fusion.4 = bf16[264,1024]{1,0:T(8,128)(2,1)} fusion(bf16[264,1024]{1,0:T(8,128)(2,1)S(1)} %fusion.6, bf16[1024,1024]{1,0:T(8,128)(2,1)S(1)} %copy-done, f32[1024]{0:T(1024)S(1)} %copy-done.9), kind=kOutput, calls=%fused_computation.10 | convolution fusion | flops 554188800 | bytes 3182592 | tf_op jit(solution)/shard_map/hk,hm->km/dot_general | solution.py:79
  82.1 2.8 %fusion.7 = bf16[264,1024]{1,0:T(8,128)(2,1)} fusion(bf16[1024,256]{1,0:T(8,128)(2,1)S(1)} %copy-done.4, bf16[264,1024]{1,0:T(8,128)(2,1)} %fusion.4, bf16[256,264]{0,1:T(8,128)(2,1)S(1)} %copy-done.6, f32[256]{0:T(256)S(1)} %copy-done.10, s32[264]{0:T(512)S(1)} %lt.30, pred[264]{0:T(512)(128)(4,1)S(1)} %and.41), kind=kOutput, calls=%fused_computation.13 | convolution fusion | flops 278648832 | bytes 1743144 | tf_op jit(solution)/shard_map/kn,nm->km/dot_general | solution.py:88
  84.9 2.0 %fusion.17 = bf16[32,264]{1,0:T(8,128)(2,1)S(1)} fusion(bf16[32,1024]{1,0:T(8,128)(2,1)S(1)} %copy-done.7, bf16[264,1024]{1,0:T(8,128)(2,1)} %fusion.7, bf16[1024,1024]{1,0:T(8,128)(2,1)S(1)} %copy-done, bf16[264,1024]{1,0:T(8,128)(2,1)S(1)} %fusion.6), kind=kOutput, calls=%fused_computation.30 | convolution fusion | flops 572309760 | bytes 3260928 | tf_op jit(solution)/shard_map/lh,hm->lm/dot_general | solution.py:94
  88.7 5.5 %all-to-all-start.2 = ((bf16[64,2,128]{2,1,0:T(2,128)(2,1)}), bf16[64,2,128]{2,1,0:T(2,128)(2,1)S(1)}, u32[]{:S(2)}, u32[]{:S(2)}) async-start(bf16[64,2,128]{2,1,0:T(2,128)(2,1)} %reshape.262), calls=%async_computation.2 | async-start | bytes 65536 | tf_op jit(solution)/shard_map/all_to_all | solution.py:173
  94.3 8.5 %all-to-all-done.2 = bf16[64,2,128]{2,1,0:T(2,128)(2,1)S(1)} async-done(((bf16[64,2,128]{2,1,0:T(2,128)(2,1)}), bf16[64,2,128]{2,1,0:T(2,128)(2,1)S(1)}, u32[]{:S(2)}, u32[]{:S(2)}) %all-to-all-start.2) | async-done | bytes 32800 | tf_op jit(solution)/shard_map/all_to_all | solution.py:173
  104.1 1.9 %collective-permute-start.4 = (f32[16,32,16]{2,1,0:T(8,128)S(1)}, f32[16,32,16]{2,1,0:T(8,128)S(1)}, u32[]{:S(2)}, u32[]{:S(2)}) collective-permute-start(f32[16,32,16]{2,1,0:T(8,128)S(1)} %get-tuple-element.7), channel_id=1, source_target_pairs={{0,1},{1,2},{2,3},{3,4},{4,5},{5,6},{6,7},{7,8},{8,9},{9,10},{10,1... | collective-permute-start | bytes 98312 | tf_op jit(solution)/shard_map/ppermute | solution.py:20
  106.0 5.6 %collective-permute-start.5 = (f32[16,32,16]{2,1,0:T(8,128)S(1)}, f32[16,32,16]{2,1,0:T(8,128)S(1)}, u32[]{:S(2)}, u32[]{:S(2)}) collective-permute-start(f32[16,32,16]{2,1,0:T(8,128)S(1)} %get-tuple-element.8), channel_id=1, source_target_pairs={{1,0},{2,1},{3,2},{4,3},{5,4},{6,5},{7,6},{8,7},{9,8},{10,9},{11,1... | collective-permute-start | bytes 98312 | tf_op jit(solution)/shard_map/ppermute | solution.py:23
  111.6 4.4 %collective-permute-done.4 = f32[16,32,16]{2,1,0:T(8,128)S(1)} collective-permute-done((f32[16,32,16]{2,1,0:T(8,128)S(1)}, f32[16,32,16]{2,1,0:T(8,128)S(1)}, u32[]{:S(2)}, u32[]{:S(2)}) %collective-permute-start.4) | collective-permute-done | bytes 32800 | tf_op jit(solution)/shard_map/ppermute | solution.py:20
  118.7 2.6 %collective-permute-start.7 = (f32[16,32,128]{2,1,0:T(8,128)S(1)}, f32[16,32,128]{2,1,0:T(8,128)S(1)}, u32[]{:S(2)}, u32[]{:S(2)}) collective-permute-start(f32[16,32,128]{2,1,0:T(8,128)S(1)} %fusion.28), channel_id=1, source_target_pairs={{12,0},{24,12},{36,24},{48,36},{60,48},{72,60},{84,72},{96,84},{10... | collective-permute-start | bytes 786440 | tf_op jit(solution)/shard_map/ppermute | solution.py:23
  121.3 1.9 %collective-permute-start.6 = (f32[16,32,128]{2,1,0:T(8,128)S(1)}, f32[16,32,128]{2,1,0:T(8,128)S(1)}, u32[]{:S(2)}, u32[]{:S(2)}) collective-permute-start(f32[16,32,128]{2,1,0:T(8,128)S(1)} %fusion.28), channel_id=1, source_target_pairs={{0,12},{12,24},{24,36},{36,48},{48,60},{60,72},{72,84},{84,96},{96... | collective-permute-start | bytes 786440 | tf_op jit(solution)/shard_map/ppermute | solution.py:20
  123.2 1.9 %collective-permute-done.7 = f32[16,32,128]{2,1,0:T(8,128)S(1)} collective-permute-done((f32[16,32,128]{2,1,0:T(8,128)S(1)}, f32[16,32,128]{2,1,0:T(8,128)S(1)}, u32[]{:S(2)}, u32[]{:S(2)}) %collective-permute-start.7) | collective-permute-done | bytes 262176 | tf_op jit(solution)/shard_map/ppermute | solution.py:23
  125.2 5.9 %collective-permute-done.6 = f32[16,32,128]{2,1,0:T(8,128)S(1)} collective-permute-done((f32[16,32,128]{2,1,0:T(8,128)S(1)}, f32[16,32,128]{2,1,0:T(8,128)S(1)}, u32[]{:S(2)}, u32[]{:S(2)}) %collective-permute-start.6) | collective-permute-done | bytes 262176 | tf_op jit(solution)/shard_map/ppermute | solution.py:20
  (83 shorter events, 25.5 us)
Async XLA Ops:
  0.0 80.5 %copy-start = (bf16[1024,1024]{1,0:T(8,128)(2,1)S(1)}, bf16[1024,1024]{1,0:T(8,128)(2,1)}, u32[]{:S(2)}) copy-start(bf16[1024,1024]{1,0:T(8,128)(2,1)} %param.22) | copy-start | bytes 6291460
  1.3 30.0 %collective-permute-start = (f32[16,32,128]{2,0,1:T(8,128)S(1)}, f32[16,32,128]{2,0,1:T(8,128)S(1)}, u32[]{:S(2)}, u32[]{:S(2)}) collective-permute-start(f32[16,32,128]{2,0,1:T(8,128)S(1)} %copy.115), channel_id=1, source_target_pairs={{0,12},{12,24},{24,36},{36,48},{48,60},{60,72},{72,84},{84,96},{96... | collective-permute-start | bytes 786440 | tf_op jit(solution)/shard_map/ppermute | solution.py:20
  3.2 28.0 %collective-permute-start.1 = (f32[16,32,128]{2,0,1:T(8,128)S(1)}, f32[16,32,128]{2,0,1:T(8,128)S(1)}, u32[]{:S(2)}, u32[]{:S(2)}) collective-permute-start(f32[16,32,128]{2,0,1:T(8,128)S(1)} %copy.115), channel_id=1, source_target_pairs={{12,0},{24,12},{36,24},{48,36},{60,48},{72,60},{84,72},{96,84},{10... | collective-permute-start | bytes 786440 | tf_op jit(solution)/shard_map/ppermute | solution.py:23
  11.4 17.9 %all-to-all-start = ((bf16[64,1,1]{2,1,0:T(2,128)(2,1)}), bf16[64,1,1]{2,1,0:T(2,128)(2,1)S(1)}, u32[]{:S(2)}, u32[]{:S(2)}) async-start(bf16[64,1,1]{2,1,0:T(2,128)(2,1)} %copy.94), calls=%async_computation | async-start | bytes 65536 | tf_op jit(solution)/shard_map/all_to_all | solution.py:146
  31.2 17.3 %copy-start.3 = (s32[64]{0:T(128)}, s32[64]{0:T(128)S(1)}, u32[]{:S(2)}) copy-start(s32[64]{0:T(128)S(1)} %get-tuple-element.6) | copy-start | bytes 772
  31.9 20.9 %collective-permute-start.2 = (f32[16,32,16]{2,0,1:T(8,128)S(1)}, f32[16,32,16]{2,0,1:T(8,128)S(1)}, u32[]{:S(2)}, u32[]{:S(2)}) collective-permute-start(f32[16,32,16]{2,0,1:T(8,128)S(1)} %get-tuple-element.9), channel_id=1, source_target_pairs={{0,1},{1,2},{2,3},{3,4},{4,5},{5,6},{6,7},{7,8},{8,9},{9,10},{10,1... | collective-permute-start | bytes 98312 | tf_op jit(solution)/shard_map/ppermute | solution.py:20
  36.2 17.8 %collective-permute-start.3 = (f32[16,32,16]{2,0,1:T(8,128)S(1)}, f32[16,32,16]{2,0,1:T(8,128)S(1)}, u32[]{:S(2)}, u32[]{:S(2)}) collective-permute-start(f32[16,32,16]{2,0,1:T(8,128)S(1)} %get-tuple-element.10), channel_id=1, source_target_pairs={{1,0},{2,1},{3,2},{4,3},{5,4},{6,5},{7,6},{8,7},{9,8},{10,9},{11,1... | collective-permute-start | bytes 98312 | tf_op jit(solution)/shard_map/ppermute | solution.py:23
  49.2 5.1 %copy-start.2 = (f32[160,128]{1,0:T(8,128)S(1)}, f32[160,128]{1,0:T(8,128)}, u32[]{:S(2)}) copy-start(f32[160,128]{1,0:T(8,128)} %negate_multiply_fusion) | copy-start | bytes 245764
  49.2 5.1 %copy-start.5 = (f32[16,32,128]{2,1,0:T(8,128)S(1)}, f32[16,32,128]{2,1,0:T(8,128)}, u32[]{:S(2)}) copy-start(f32[16,32,128]{2,1,0:T(8,128)} %param.14) | copy-start | bytes 786436
  60.5 19.7 %copy-start.7 = (bf16[32,1024]{1,0:T(8,128)(2,1)S(1)}, bf16[32,1024]{1,0:T(8,128)(2,1)}, u32[]{:S(2)}) copy-start(bf16[32,1024]{1,0:T(8,128)(2,1)} %param.20) | copy-start | bytes 196612
  60.5 19.7 %copy-start.8 = (f32[1024]{0:T(1024)S(1)}, f32[1024]{0:T(1024)}, u32[]{:S(2)}) copy-start(f32[1024]{0:T(1024)} %param.21) | copy-start | bytes 12292
  60.5 20.0 %copy-start.9 = (f32[1024]{0:T(1024)S(1)}, f32[1024]{0:T(1024)}, u32[]{:S(2)}) copy-start(f32[1024]{0:T(1024)} %param.23) | copy-start | bytes 12292
  63.5 16.2 %all-to-all-start.1 = ((bf16[64,2,128]{2,1,0:T(2,128)(2,1)}), bf16[64,2,128]{2,1,0:T(2,128)(2,1)S(1)}, u32[]{:S(2)}, u32[]{:S(2)}) async-start(bf16[64,2,128]{2,1,0:T(2,128)(2,1)} %reshape.260), calls=%async_computation.1 | async-start | bytes 65536 | tf_op jit(solution)/shard_map/all_to_all | solution.py:145
  80.5 1.6 %copy-start.4 = (bf16[1024,256]{1,0:T(8,128)(2,1)S(1)}, bf16[1024,256]{1,0:T(8,128)(2,1)}, u32[]{:S(2)}) copy-start(bf16[1024,256]{1,0:T(8,128)(2,1)} %param.24) | copy-start | bytes 1572868
  80.5 1.6 %copy-start.6 = (bf16[256,264]{0,1:T(8,128)(2,1)S(1)}, bf16[256,264]{0,1:T(8,128)(2,1)}, u32[]{:S(2)}) copy-start(bf16[256,264]{0,1:T(8,128)(2,1)} %param.19) | copy-start | bytes 405508
  80.5 1.6 %copy-start.10 = (f32[256]{0:T(256)S(1)}, f32[256]{0:T(256)}, u32[]{:S(2)}) copy-start(f32[256]{0:T(256)} %param.25) | copy-start | bytes 3076
  88.7 14.1 %all-to-all-start.2 = ((bf16[64,2,128]{2,1,0:T(2,128)(2,1)}), bf16[64,2,128]{2,1,0:T(2,128)(2,1)S(1)}, u32[]{:S(2)}, u32[]{:S(2)}) async-start(bf16[64,2,128]{2,1,0:T(2,128)(2,1)} %reshape.262), calls=%async_computation.2 | async-start | bytes 65536 | tf_op jit(solution)/shard_map/all_to_all | solution.py:173
  103.6 13.6 %copy-start.11 = (f32[16]{0:T(128)S(1)}, f32[16]{0:T(128)}, u32[]{:S(2)}) copy-start(f32[16]{0:T(128)} %get-tuple-element.11) | copy-start | bytes 196
  103.6 13.6 %copy-start.12 = (f32[16]{0:T(128)S(1)}, f32[16]{0:T(128)}, u32[]{:S(2)}) copy-start(f32[16]{0:T(128)} %sqrt.13) | copy-start | bytes 196
  104.1 11.9 %collective-permute-start.4 = (f32[16,32,16]{2,1,0:T(8,128)S(1)}, f32[16,32,16]{2,1,0:T(8,128)S(1)}, u32[]{:S(2)}, u32[]{:S(2)}) collective-permute-start(f32[16,32,16]{2,1,0:T(8,128)S(1)} %get-tuple-element.7), channel_id=1, source_target_pairs={{0,1},{1,2},{2,3},{3,4},{4,5},{5,6},{6,7},{7,8},{8,9},{9,10},{10,1... | collective-permute-start | bytes 98312 | tf_op jit(solution)/shard_map/ppermute | solution.py:20
  106.0 11.2 %collective-permute-start.5 = (f32[16,32,16]{2,1,0:T(8,128)S(1)}, f32[16,32,16]{2,1,0:T(8,128)S(1)}, u32[]{:S(2)}, u32[]{:S(2)}) collective-permute-start(f32[16,32,16]{2,1,0:T(8,128)S(1)} %get-tuple-element.8), channel_id=1, source_target_pairs={{1,0},{2,1},{3,2},{4,3},{5,4},{6,5},{7,6},{8,7},{9,8},{10,9},{11,1... | collective-permute-start | bytes 98312 | tf_op jit(solution)/shard_map/ppermute | solution.py:23
  118.7 12.4 %copy-start.1 = (f32[16,32,128]{2,1,0:T(8,128)S(1)}, f32[16,32,128]{2,1,0:T(8,128)}, u32[]{:S(2)}) copy-start(f32[16,32,128]{2,1,0:T(8,128)} %param.13) | copy-start | bytes 786436
  118.7 6.4 %collective-permute-start.7 = (f32[16,32,128]{2,1,0:T(8,128)S(1)}, f32[16,32,128]{2,1,0:T(8,128)S(1)}, u32[]{:S(2)}, u32[]{:S(2)}) collective-permute-start(f32[16,32,128]{2,1,0:T(8,128)S(1)} %fusion.28), channel_id=1, source_target_pairs={{12,0},{24,12},{36,24},{48,36},{60,48},{72,60},{84,72},{96,84},{10... | collective-permute-start | bytes 786440 | tf_op jit(solution)/shard_map/ppermute | solution.py:23
  121.3 9.8 %collective-permute-start.6 = (f32[16,32,128]{2,1,0:T(8,128)S(1)}, f32[16,32,128]{2,1,0:T(8,128)S(1)}, u32[]{:S(2)}, u32[]{:S(2)}) collective-permute-start(f32[16,32,128]{2,1,0:T(8,128)S(1)} %fusion.28), channel_id=1, source_target_pairs={{0,12},{12,24},{24,36},{36,48},{48,60},{60,72},{72,84},{84,96},{96... | collective-permute-start | bytes 786440 | tf_op jit(solution)/shard_map/ppermute | solution.py:20
where the time goes:
time: 134 us; the launch traced here: 133 us
  starting transfers between devices  58.6 us (44%)
  waiting for transfers between devices  36.7 us (27%)
  matrix products  13.7 us (10%)
  local copies, waits for them, and re-layouts  13 us (10%)
  other arithmetic  9.94 us (7%)
    ppermute x4, starting transfers between devices, padded_2(): lax.ppermute(lax.slice_in_dim(block, 0, width, axis=dim), axis, backward)  26.1 us
    ppermute x4, waiting for transfers between devices, padded_2(): lax.ppermute(lax.slice_in_dim(block, block.shape[dim] - width, None, axis...  13.2 us
    ppermute x4, starting transfers between devices, padded_2(): lax.ppermute(lax.slice_in_dim(block, block.shape[dim] - width, None, axis...  10 us
    all_to_all x1, starting transfers between devices, observe(): lax.all_to_all(slot_flags, 'lat', split_axis=0, concat_axis=0, tiled=True)  9.32 us
    all_to_all x1, waiting for transfers between devices, observe(): lax.all_to_all(returning.reshape(lat_count, send_cap, block_size), 'lat',...  8.5 us
    all_to_all x1, waiting for transfers between devices, observe(): lax.all_to_all(outgoing, 'lat', split_axis=0, concat_axis=0, tiled=True)  7.72 us
    all_to_all x1, starting transfers between devices, observe(): lax.all_to_all(outgoing, 'lat', split_axis=0, concat_axis=0, tiled=True)  7.62 us
    all_to_all x1, starting transfers between devices, observe(): lax.all_to_all(returning.reshape(lat_count, send_cap, block_size), 'lat',...  5.5 us
  transfers between devices with their start and end apart: 11, of which 9 were waited for; matrix products, arithmetic and copies ran while one was open for 9% of the time, Pallas kernels for 0%

commit v1 on v0

v1 whole, which is shorter than its diff:
```python
import functools

import jax
import jax.numpy as jnp
import numpy as np
from jax import lax
from jax.experimental import pallas as pl
from jax.experimental.pallas import tpu as pltpu
from jax.sharding import PartitionSpec as P

REACH = 16
BLOCK_COLS = 8
LAT_SIGMA = 8.0
UNSEEN = 32768.0
MESH = pl.DeviceIdType.MESH
F32 = jnp.float32
BF16 = jnp.bfloat16
I32 = jnp.int32
NN = (((1,), (0,)), ((), ()))
NT = (((1,), (1,)), ((), ()))

steps = np.arange(-REACH, REACH + 1).astype(np.float64)
raw = np.exp(-steps * steps / (2.0 * LAT_SIGMA**2))
LAT_TAPS = [float(v) for v in raw / np.sqrt(np.sum(raw * raw))]
LAT_NORM = float(1.0 / np.sqrt(np.sum(raw * raw)))


def dot(a, b, dims=NN):
    return lax.dot_general(a, b, dims, preferred_element_type=F32)


def split_two(value):
    high = value.astype(BF16)
    return high, (value - high.astype(F32)).astype(BF16)


def iota(shape, dim):
    return lax.broadcasted_iota(I32, shape, dim)


def smooth_rows(above, here, below, keep_above, keep_below, height, levels, store):
    def tile(t, carry):
        at = pl.ds(pl.multiple_of(t * 8, 8), 8)
        rows = [above[r, at, :] * keep_above for r in range(height)]
        rows += [here[r, at, :] for r in range(height)]
        rows += [below[r, at, :] * keep_below for r in range(height)]
        for r in range(height):
            total = rows[r + REACH] * LAT_TAPS[REACH]
            for j in range(1, REACH + 1):
                total += (rows[r + REACH - j] + rows[r + REACH + j]) * LAT_TAPS[REACH + j]
            store(r, at, total)
        return carry

    lax.fori_loop(0, levels // 8, tile, 0)


def kernel(
    n_lat,
    n_lon,
    control_hbm,
    background_hbm,
    width_ref,
    cells_ref,
    owner_ref,
    count_ref,
    radiance_hbm,
    w1_hbm,
    b1_ref,
    w2_hbm,
    b2_ref,
    w3_hbm,
    b3_ref,
    out_ref,
    control,
    background,
    radiance,
    w1,
    w2,
    w3,
    above,
    below,
    pack,
    from_left,
    from_right,
    flags,
    outgoing,
    observed,
    smooth,
    split_rows,
    split_back,
    rims,
    taps_high,
    taps_low,
    picks,
    band_high,
    band_low,
    back_rows,
    slot_rows,
    act_one,
    act_two,
    grad_two,
    grad_one,
    emitted,
    landed,
    landed_send,
    rim_send,
    above_back,
    below_back,
    left_back,
    right_back,
    local_sem,
    flag_send,
    flag_recv,
    rad_send,
    rad_recv,
    halo_send,
    halo_recv,
    back_send,
    back_recv,
):
    height, levels, width = control.shape
    slots = n_lat * BLOCK_COLS
    main = height * width
    side = height * REACH
    me = lax.axis_index("lat")
    col = lax.axis_index("lon")
    lat_at = {d: lax.rem(me + d + n_lat, n_lat) for d in (-1, 0, 1)}
    lon_at = {d: lax.rem(col + d + n_lon, n_lon) for d in (-1, 1)}

    barrier = pltpu.get_barrier_semaphore()
    for dl in (-1, 0, 1):
        for dq in (-1, 1):
            pl.semaphore_signal(
                barrier, inc=1, device_id=(lat_at[dl], lon_at[dq]), device_id_type=MESH
            )

    def greet(d, carry):
        pl.semaphore_signal(
            barrier, inc=1, device_id=(lax.rem(me + d, n_lat), col), device_id_type=MESH
        )
        return carry

    lax.fori_loop(1, n_lat, greet, 0)

    loads = [
        pltpu.make_async_copy(source, target, local_sem.at[k])
        for k, (source, target) in enumerate(
            (
                (control_hbm, control),
                (background_hbm, background),
                (radiance_hbm, radiance),
                (w1_hbm, w1),
                (w2_hbm, w2),
                (w3_hbm, w3),
            )
        )
    ]
    for load in loads:
        load.start()

    n_slots = owner_ref.shape[1]
    diag = iota((n_slots, n_slots), 0) == iota((n_slots, n_slots), 1)

    def upright(row):
        return jnp.sum(jnp.where(diag, row, 0), axis=1, keepdims=True)

    owner_col = upright(owner_ref[...])
    cells_col = upright(cells_ref[...])
    flags[pl.ds(me, 1)] = jnp.sum(
        (owner_col == iota((n_slots, 128), 1)).astype(F32), axis=0, keepdims=True
    ).reshape(1, 1, 128)

    loads[0].wait()
    lane = iota((levels, width), 1)
    per = width // REACH
    for k, start in enumerate((0, width - REACH)):
        for group in range(height // per):
            packed = jnp.zeros((levels, width), F32)
            for r in range(per):
                shift = (r * REACH - start) % width
                value = control[group * per + r]
                value = pltpu.roll(value, shift, 1) if shift else value
                packed = jnp.where(lane // REACH == r, value, packed)
            pack[k, group] = packed

    pl.semaphore_wait(barrier, n_lat - 1 + 6)

    def rim_copies(main_src, above_dst, below_dst, left_src, right_src, left_dst, right_dst, send, recv):
        copies = [
            pltpu.make_async_remote_copy(
                main_src, below_dst, send.at[0], recv.at[0], (lat_at[-1], col), MESH
            ),
            pltpu.make_async_remote_copy(
                main_src, above_dst, send.at[1], recv.at[1], (lat_at[1], col), MESH
            ),
        ]
        for dl in (-1, 0, 1):
            k = 2 + dl + 1
            copies.append(
                pltpu.make_async_remote_copy(
                    left_src, right_dst.at[1 - dl], send.at[k], recv.at[k],
                    (lat_at[dl], lon_at[-1]), MESH,
                )
            )
            copies.append(
                pltpu.make_async_remote_copy(
                    right_src, left_dst.at[1 - dl], send.at[k + 3], recv.at[k + 3],
                    (lat_at[dl], lon_at[1]), MESH,
                )
            )
        return copies

    def flag_copy(d):
        return pltpu.make_async_remote_copy(
            flags.at[me], flags.at[me], flag_send.at[d], flag_recv.at[d],
            (lax.rem(me + d, n_lat), col), MESH,
        )

    def rad_copy(d):
        target = lax.rem(me + d, n_lat)
        return pltpu.make_async_remote_copy(
            outgoing.at[target], observed.at[me], rad_send.at[d], rad_recv.at[d],
            (target, col), MESH,
        )

    def each(step):
        def body(d, carry):
            step(d)
            return carry

        lax.fori_loop(1, n_lat, body, 0)

    each(lambda d: flag_copy(d).start())
    halo = rim_copies(
        control, above, below, pack.at[0], pack.at[1], from_left, from_right, halo_send, halo_recv
    )
    for copy in halo:
        copy.start()

    mine = owner_col == iota((n_slots, slots), 1) // BLOCK_COLS
    cell = jnp.sum(jnp.where(mine, cells_col, 0), axis=0, keepdims=True)
    live = jnp.sum(mine.astype(F32), axis=0, keepdims=True)
    groups = width // BLOCK_COLS
    row_of = cell // groups
    lane_x = iota((1, slots), 1)
    place = (cell - row_of * groups) * BLOCK_COLS + lane_x % BLOCK_COLS
    spread = jnp.zeros((1, slots), F32)
    for r in range(height):
        spread += jnp.where(row_of == r, width_ref[r].astype(F32), 0.0)
    offset = iota((40, slots), 0).astype(F32) - REACH
    squares = jnp.sum(
        jnp.where(offset <= REACH, jnp.exp(-offset * offset / (spread * spread)), 0.0),
        axis=0,
        keepdims=True,
    )
    scale = live / jnp.sqrt(squares)
    rate = -0.5 / (spread * spread)

    def taps_at(column):
        away = (column - place).astype(F32)
        return jnp.where(jnp.abs(away) <= REACH, jnp.exp(away * away * rate) * scale, 0.0)

    column = iota((width, slots), 0)
    tap_high, tap_low = split_two(taps_at(column))
    pick = jnp.where(column == place, live, 0.0).astype(BF16)

    def lay(r, carry):
        rows = pl.ds(pl.multiple_of(r * width, width), width)
        keep = jnp.where(row_of == r, 1.0, 0.0).astype(BF16)
        taps_high[rows, :] = tap_high * keep
        taps_low[rows, :] = tap_low * keep
        picks[rows, :] = pick * keep
        return carry

    lax.fori_loop(0, height, lay, 0)
    rim = iota((side, slots), 0)
    for k, start in enumerate((-REACH, width)):
        value = jnp.where(rim // REACH == row_of, taps_at(rim % REACH + start), 0.0)
        high, low = split_two(value)
        taps_high[pl.ds(main + k * side, side), :] = high
        taps_low[pl.ds(main + k * side, side), :] = low

    rim_in = iota((3 * side, side), 0)
    rim_out = iota((3 * side, side), 1)
    away = (rim_in // REACH - height - rim_out // REACH).astype(F32)
    band = jnp.exp(away * away * (-0.5 / LAT_SIGMA**2)) * LAT_NORM
    band = jnp.where((jnp.abs(away) <= REACH) & (rim_in % REACH == rim_out % REACH), band, 0.0)
    high, low = split_two(band)
    band_high[...] = high
    band_low[...] = low

    loads[1].wait()
    for r in range(height):
        value = background[r]
        high, rest = split_two(value)
        middle = rest
        low = (value - high.astype(F32) - middle.astype(F32)).astype(BF16)
        lanes = pl.ds(r * width, width)
        split_back[pl.ds(0, levels), lanes] = high
        split_back[pl.ds(levels, levels), lanes] = middle
        split_back[pl.ds(2 * levels, levels), lanes] = low
    gathered = dot(split_back[...], picks[...])
    back_rows[...] = (
        gathered[:levels] + gathered[levels : 2 * levels] + gathered[2 * levels :]
    )

    loads[2].wait()
    n_recv = radiance.shape[0] // BLOCK_COLS
    channels = radiance.shape[1]
    counts = jnp.sum(
        jnp.where(
            iota((n_recv * BLOCK_COLS, n_recv), 1)
            == iota((n_recv * BLOCK_COLS, n_recv), 0) // BLOCK_COLS,
            count_ref[...],
            0,
        ),
        axis=1,
        keepdims=True,
    )
    seen = jnp.where(
        iota((n_recv * BLOCK_COLS, channels), 1) < counts, radiance[...].astype(F32), UNSEEN
    ).astype(BF16)

    each(lambda d: flag_copy(d).wait_recv())
    table = flags[...].reshape(n_lat, 128)
    sent = jnp.sum(
        jnp.where(iota((n_lat, 128), 1) == me, table, 0.0), axis=1, keepdims=True
    )
    sent = jnp.broadcast_to(sent, (n_lat, n_recv * BLOCK_COLS)).astype(BF16)
    source = iota((slots, n_lat), 0) // BLOCK_COLS
    entry = iota((slots, n_lat), 1)
    present = dot((entry == source).astype(BF16), sent)
    arrival = dot((entry < source).astype(BF16), sent)
    slot_x = iota((slots, n_recv * BLOCK_COLS), 1)
    row_x = iota((slots, n_recv * BLOCK_COLS), 0)
    select = (
        (present > 0.5)
        & (arrival == (slot_x // BLOCK_COLS).astype(F32))
        & (slot_x % BLOCK_COLS == row_x % BLOCK_COLS)
    )
    outgoing[...] = (
        dot(select.astype(BF16), seen).reshape(n_lat, BLOCK_COLS, channels).astype(BF16)
    )
    own = pltpu.make_async_copy(outgoing.at[me], observed.at[me], local_sem.at[6])
    own.start()
    each(lambda d: rad_copy(d).start())

    keep_above = jnp.where(me > 0, 1.0, 0.0).astype(F32)
    keep_below = jnp.where(me < n_lat - 1, 1.0, 0.0).astype(F32)
    for copy in halo:
        copy.wait_recv()

    def keep_smooth(r, at, value):
        smooth[r, at, :] = value

    smooth_rows(above, control, below, keep_above, keep_below, height, levels, keep_smooth)
    for r in range(height):
        high, low = split_two(smooth[r])
        split_rows[pl.ds(0, levels), pl.ds(r * width, width)] = high
        split_rows[pl.ds(levels, levels), pl.ds(r * width, width)] = low
    keeps = (keep_above, 1.0, keep_below)
    for k, ref in enumerate((from_left, from_right)):
        for b in range(3):
            for g in range(side // width):
                high, low = split_two(ref[b, g] * keeps[b])
                lanes = pl.ds(b * side + g * width, width)
                rims[pl.ds(k * levels, levels), lanes] = high
                rims[pl.ds((2 + k) * levels, levels), lanes] = low
    crossed = dot(rims[...], band_high[...])
    crossed = (
        crossed[: 2 * levels]
        + crossed[2 * levels :]
        + dot(rims[pl.ds(0, 2 * levels), :], band_low[...])
    )
    for k in range(2):
        high, low = split_two(crossed[k * levels : (k + 1) * levels])
        lanes = pl.ds(main + k * side, side)
        split_rows[pl.ds(0, levels), lanes] = high
        split_rows[pl.ds(levels, levels), lanes] = low
    total = dot(split_rows[...], taps_high[...])
    profile = (
        total[:levels]
        + total[levels:]
        + dot(split_rows[pl.ds(0, levels), :], taps_low[...])
        + back_rows[...]
    )
    slot_rows[...] = profile.T.astype(BF16)

    for load in loads[3:]:
        load.wait()
    tile = 256
    hidden = w2.shape[0]

    def lanes_of(n):
        return pl.ds(pl.multiple_of(n * tile, tile), tile)

    def first(n, carry):
        at = lanes_of(n)
        act_one[:, at] = jnp.tanh(dot(slot_rows[...], w1[:, at]) + b1_ref[:, at]).astype(BF16)
        return carry

    def second(n, carry):
        at = lanes_of(n)
        act_two[:, at] = jnp.tanh(dot(act_one[...], w2[:, at]) + b2_ref[:, at]).astype(BF16)
        return carry

    lax.fori_loop(0, hidden // tile, first, 0)
    lax.fori_loop(0, hidden // tile, second, 0)
    emitted[...] = dot(act_two[...], w3[...]) + b3_ref[...]

    own.wait()
    each(lambda d: rad_copy(d).wait_recv())
    target = observed[...].astype(F32).reshape(slots, channels)
    misfit = jnp.where(target < 0.5 * UNSEEN, emitted[...] - target, 0.0).astype(BF16)

    def second_back(n, carry):
        at = lanes_of(n)
        value = act_two[:, at].astype(F32)
        grad_two[:, at] = (dot(misfit, w3[at, :], NT) * (1.0 - value * value)).astype(BF16)
        return carry

    def first_back(n, carry):
        at = lanes_of(n)
        value = act_one[:, at].astype(F32)
        grad_one[:, at] = (dot(grad_two[...], w2[at, :], NT) * (1.0 - value * value)).astype(BF16)
        return carry

    lax.fori_loop(0, hidden // tile, second_back, 0)
    lax.fori_loop(0, hidden // tile, first_back, 0)
    sensitivity = dot(w1[...], grad_one[...], NT).astype(BF16)

    spreadout = dot(sensitivity, taps_high[...], NT)
    for r in range(height):
        value = spreadout[:, r * width : (r + 1) * width]
        landed[r] = value
        landed_send[r] = value.astype(BF16)
    for k in range(2):
        rim_send[k] = spreadout[:, main + k * side : main + (k + 1) * side].astype(BF16)
    back = rim_copies(
        landed_send, above_back, below_back, rim_send.at[0], rim_send.at[1],
        left_back, right_back, back_send, back_recv,
    )
    for copy in back:
        copy.start()
    for copy in back:
        copy.wait_recv()

    for r in range(height):
        above[r] = above_back[r].astype(F32)
        below[r] = below_back[r].astype(F32)
    for k, ref in enumerate((left_back, right_back)):
        for b in range(3):
            rims[pl.ds(k * levels, levels), pl.ds(b * side, side)] = (
                ref[b].astype(F32) * keeps[b]
            ).astype(BF16)
    crossed = dot(rims[pl.ds(0, 2 * levels), :], band_high[...])
    for r in range(height):
        at = slice(r // per * width, (r // per + 1) * width)
        value = control[r]
        low_cols = crossed[:levels, at]
        high_cols = crossed[levels:, at]
        shift = (-(r % per) * REACH) % width
        low_cols = pltpu.roll(low_cols, shift, 1) if shift else low_cols
        shift = (width - REACH - (r % per) * REACH) % width
        high_cols = pltpu.roll(high_cols, shift, 1) if shift else high_cols
        value += jnp.where(lane < REACH, low_cols, 0.0)
        value += jnp.where(lane >= width - REACH, high_cols, 0.0)
        smooth[r] = value

    def finish(r, at, value):
        out_ref[r, at, :] = smooth[r, at, :] + value

    smooth_rows(above, landed, below, keep_above, keep_below, height, levels, finish)

    each(lambda d: flag_copy(d).wait_send())
    each(lambda d: rad_copy(d).wait_send())
    for copy in halo + back:
        copy.wait_send()


def shards(
    n_lat,
    n_lon,
    control,
    background,
    lon_width,
    block_cells,
    block_owner,
    channel_count,
    radiance,
    in_weight,
    in_bias,
    mid_weight,
    mid_bias,
    out_weight,
    out_bias,
):
    height, levels, width = control.shape
    hidden = mid_weight.shape[0]
    channels, recv_cols = radiance.shape
    slots = n_lat * BLOCK_COLS
    main = height * width
    side = height * REACH
    per_side = side // width
    dma = pltpu.SemaphoreType.DMA
    vmem = pltpu.VMEM
    any_spec = pl.BlockSpec(memory_space=pl.ANY)
    vmem_spec = pl.BlockSpec(memory_space=pltpu.VMEM)
    smem_spec = pl.BlockSpec(memory_space=pltpu.SMEM)
    grid = (height, levels, width)
    return pl.pallas_call(
        functools.partial(kernel, n_lat, n_lon),
        out_shape=jax.ShapeDtypeStruct(grid, F32),
        in_specs=[
            any_spec, any_spec, smem_spec, vmem_spec, vmem_spec, vmem_spec, any_spec,
            any_spec, vmem_spec, any_spec, vmem_spec, any_spec, vmem_spec,
        ],
        out_specs=vmem_spec,
        scratch_shapes=[
            vmem(grid, F32),
            vmem(grid, F32),
            vmem((recv_cols, channels), BF16),
            vmem((levels, hidden), BF16),
            vmem((hidden, hidden), BF16),
            vmem((hidden, channels), BF16),
            vmem(grid, F32),
            vmem(grid, F32),
            vmem((2, per_side, levels, width), F32),
            vmem((3, per_side, levels, width), F32),
            vmem((3, per_side, levels, width), F32),
            vmem((n_lat, 1, 128), F32),
            vmem((n_lat, BLOCK_COLS, channels), BF16),
            vmem((n_lat, BLOCK_COLS, channels), BF16),
            vmem(grid, F32),
            vmem((2 * levels, main + 2 * side), BF16),
            vmem((3 * levels, main), BF16),
            vmem((4 * levels, 3 * side), BF16),
            vmem((main + 2 * side, slots), BF16),
            vmem((main + 2 * side, slots), BF16),
            vmem((main, slots), BF16),
            vmem((3 * side, side), BF16),
            vmem((3 * side, side), BF16),
            vmem((levels, slots), F32),
            vmem((slots, levels), BF16),
            vmem((slots, hidden), BF16),
            vmem((slots, hidden), BF16),
            vmem((slots, hidden), BF16),
            vmem((slots, hidden), BF16),
            vmem((slots, channels), F32),
            vmem(grid, F32),
            vmem(grid, BF16),
            vmem((2, levels, side), BF16),
            vmem(grid, BF16),
            vmem(grid, BF16),
            vmem((3, levels, side), BF16),
            vmem((3, levels, side), BF16),
            dma((8,)),
            dma((n_lat,)),
            dma((n_lat,)),
            dma((n_lat,)),
            dma((n_lat,)),
            dma((8,)),
            dma((8,)),
            dma((8,)),
            dma((8,)),
        ],
        compiler_params=pltpu.CompilerParams(
            collective_id=0, has_side_effects=True, vmem_limit_bytes=60 * 1024 * 1024
        ),
    )(
        control,
        background,
        lon_width,
        block_cells.T,
        block_owner.T,
        channel_count.T,
        radiance.T,
        in_weight,
        in_bias.reshape(1, -1),
        mid_weight,
        mid_bias.reshape(1, -1),
        out_weight,
        out_bias.reshape(1, -1),
    )


def solution(mesh):
    return jax.shard_map(
        functools.partial(shards, mesh.shape["lat"], mesh.shape["lon"]),
        mesh=mesh,
        in_specs=(
            P("lat", None, "lon"),
            P("lat", None, "lon"),
            P("lat"),
            P("lat", "lon"),
            P("lat", "lon"),
            P("lat", "lon"),
            P("lat", "lon"),
            P(),
            P(),
            P(),
            P(),
            P(),
            P(),
        ),
        out_specs=P("lat", None, "lon"),
        check_vma=False,
    )
```

time: 134 us -> 53.7 us (0.40)
  the two profiles are of different devices: /device:TPU:8 before, /device:TPU:1 now
where the time goes in v1:
time: 53.7 us; the launch traced here: 53.3 us
  Pallas kernels  51.6 us (96%)
  local copies, waits for them, and re-layouts  1.67 us (3%)
    pallas_call x1, Pallas kernels, shards(): pl.pallas_call(functools.partial(kernel, n_lat, n_lon), out_shape=jax.Sha...  51.6 us
    unnamed x1, local copies, waits for them, and re-layouts  1.67 us

profile of v1, /device:TPU:1, one launch (start us, length us, event | category | flops | bytes accessed | tf_op | source)
XLA Modules:
  0.0 53.3 jit_solution(12286322377435796807)
XLA Ops:
  0.0 51.6 %shard_map.127 = f32[16,32,128]{2,1,0:T(8,128)} custom-call(f32[16,32,128]{2,1,0:T(8,128)} %control_hbm.1, f32[16,32,128]{2,1,0:T(8,128)} %background_hbm.1, s32[16]{0:T(128)} %width_ref.1, s32[1,64]{1,0:T(1,128)} %bitcast.11, s32[1,64]{1,0:T(1,128)} %bitcast.12, s32[1,33]{1,0:T(1,128)} %bitcast.13, bf16[264,256]{1,0:T(8,128)(2,1)} %bitcast.7, ...), custom_call_target="tpu_custom_call" | custom-call | tf_op jit(solution)/shard_map/pallas_call | solution.py:511
  51.6 1.7 %copy.15 = f32[16,32,128]{2,1,0:T(8,128)} copy(f32[16,32,128]{2,1,0:T(8,128)} %shard_map.127) | data formatting | bytes 524288

commit v2 on v1

--- a/solution.py
+++ b/solution.py
@@ -11,6 +11,7 @@
 REACH = 16
 BLOCK_COLS = 8
 LAT_SIGMA = 8.0
+CHUNKS = 4
 UNSEEN = 32768.0
 MESH = pl.DeviceIdType.MESH
 F32 = jnp.float32
@@ -36,6 +37,17 @@
 
 def iota(shape, dim):
     return lax.broadcasted_iota(I32, shape, dim)
+
+
+def by_distance(count):
+    return sorted(range(count), key=lambda d: (min(d, count - d), d))
+
+
+def choose(index, values):
+    chosen = jnp.zeros_like(index)
+    for k, value in enumerate(values):
+        chosen = jnp.where(index == k, value, chosen)
+    return chosen
 
 
 def smooth_rows(above, here, below, keep_above, keep_below, height, levels, store):
@@ -51,7 +63,7 @@
             store(r, at, total)
         return carry
 
-    lax.fori_loop(0, levels // 8, tile, 0)
+    lax.fori_loop(0, levels // 8, tile, 0, unroll=True)
 
 
 def kernel(
@@ -59,18 +71,25 @@
     n_lon,
     control_hbm,
     background_hbm,
+    width_hbm,
+    cells_hbm,
+    owner_hbm,
+    count_hbm,
+    radiance_hbm,
+    w1_hbm,
+    b1_hbm,
+    w2_hbm,
+    b2_hbm,
+    w3_hbm,
+    b3_hbm,
+    out_ref,
     width_ref,
     cells_ref,
     owner_ref,
     count_ref,
-    radiance_hbm,
-    w1_hbm,
     b1_ref,
-    w2_hbm,
     b2_ref,
-    w3_hbm,
     b3_ref,
-    out_ref,
     control,
     background,
     radiance,
@@ -101,6 +120,7 @@
     grad_two,
     grad_one,
     emitted,
+    misfit,
     landed,
     landed_send,
     rim_send,
@@ -127,38 +147,51 @@
     lat_at = {d: lax.rem(me + d + n_lat, n_lat) for d in (-1, 0, 1)}
     lon_at = {d: lax.rem(col + d + n_lon, n_lon) for d in (-1, 1)}
 
+    n_row = 8 if n_lat % 16 == 0 else 2
+    n_far = n_lat // n_row
+    far = me // n_row
+    near = me - far * n_row
+    rings = by_distance(n_far)
+    reaches = [(df, dn) for df in rings[::-1] for dn in range(n_row) if df or dn]
+
+    def peer(df, dn):
+        return lax.rem(far + df, n_far) * n_row + lax.rem(near + dn, n_row)
+
     barrier = pltpu.get_barrier_semaphore()
+    for df, dn in reaches:
+        pl.semaphore_signal(barrier, inc=1, device_id=(peer(df, dn), col), device_id_type=MESH)
     for dl in (-1, 0, 1):
         for dq in (-1, 1):
             pl.semaphore_signal(
                 barrier, inc=1, device_id=(lat_at[dl], lon_at[dq]), device_id_type=MESH
             )
 
-    def greet(d, carry):
-        pl.semaphore_signal(
-            barrier, inc=1, device_id=(lax.rem(me + d, n_lat), col), device_id_type=MESH
-        )
-        return carry
-
-    lax.fori_loop(1, n_lat, greet, 0)
-
     loads = [
         pltpu.make_async_copy(source, target, local_sem.at[k])
         for k, (source, target) in enumerate(
             (
+                (owner_hbm, owner_ref),
+                (cells_hbm, cells_ref),
+                (width_hbm, width_ref),
                 (control_hbm, control),
                 (background_hbm, background),
+                (count_hbm, count_ref),
                 (radiance_hbm, radiance),
                 (w1_hbm, w1),
+                (b1_hbm, b1_ref),
                 (w2_hbm, w2),
+                (b2_hbm, b2_ref),
                 (w3_hbm, w3),
+                (b3_hbm, b3_ref),
             )
         )
     ]
-    for load in loads:
+    for load in loads[:4]:
         load.start()
 
     n_slots = owner_ref.shape[1]
+    for load in loads[:3]:
+        load.wait()
     diag = iota((n_slots, n_slots), 0) == iota((n_slots, n_slots), 1)
 
     def upright(row):
@@ -170,7 +203,7 @@
         (owner_col == iota((n_slots, 128), 1)).astype(F32), axis=0, keepdims=True
     ).reshape(1, 1, 128)
 
-    loads[0].wait()
+    loads[3].wait()
     lane = iota((levels, width), 1)
     per = width // REACH
     for k, start in enumerate((0, width - REACH)):
@@ -185,17 +218,10 @@
 
     pl.semaphore_wait(barrier, n_lat - 1 + 6)
 
-    def rim_copies(main_src, above_dst, below_dst, left_src, right_src, left_dst, right_dst, send, recv):
-        copies = [
-            pltpu.make_async_remote_copy(
-                main_src, below_dst, send.at[0], recv.at[0], (lat_at[-1], col), MESH
-            ),
-            pltpu.make_async_remote_copy(
-                main_src, above_dst, send.at[1], recv.at[1], (lat_at[1], col), MESH
-            ),
-        ]
+    def side_copies(left_src, right_src, left_dst, right_dst, send, recv):
+        copies = []
         for dl in (-1, 0, 1):
-            k = 2 + dl + 1
+            k = dl + 1
             copies.append(
                 pltpu.make_async_remote_copy(
                     left_src, right_dst.at[1 - dl], send.at[k], recv.at[k],
@@ -210,34 +236,44 @@
             )
         return copies
 
-    def flag_copy(d):
+    def band_copies(source, above_dst, below_dst, send, recv, k):
+        return [
+            pltpu.make_async_remote_copy(
+                source, below_dst, send.at[k], recv.at[k], (lat_at[-1], col), MESH
+            ),
+            pltpu.make_async_remote_copy(
+                source, above_dst, send.at[k + 1], recv.at[k + 1], (lat_at[1], col), MESH
+            ),
+        ]
+
+    flag_copies = [
+        pltpu.make_async_remote_copy(
+            flags.at[me], flags.at[me], flag_send.at[df * n_row + dn],
+            flag_recv.at[df * n_row + dn], (peer(df, dn), col), MESH,
+        )
+        for df, dn in reaches
+    ]
+
+    def rad_copy(df, dn):
+        source = rings[::-1].index(df) * n_row + lax.rem(near + dn, n_row)
+        place = rings.index((n_far - df) % n_far) * n_row + near
         return pltpu.make_async_remote_copy(
-            flags.at[me], flags.at[me], flag_send.at[d], flag_recv.at[d],
-            (lax.rem(me + d, n_lat), col), MESH,
+            outgoing.at[source], observed.at[place], rad_send.at[df * n_row + dn],
+            rad_recv.at[df * n_row + dn], (peer(df, dn), col), MESH,
         )
 
-    def rad_copy(d):
-        target = lax.rem(me + d, n_lat)
-        return pltpu.make_async_remote_copy(
-            outgoing.at[target], observed.at[me], rad_send.at[d], rad_recv.at[d],
-            (target, col), MESH,
-        )
-
-    def each(step):
-        def body(d, carry):
-            step(d)
-            return carry
-
-        lax.fori_loop(1, n_lat, body, 0)
-
-    each(lambda d: flag_copy(d).start())
-    halo = rim_copies(
-        control, above, below, pack.at[0], pack.at[1], from_left, from_right, halo_send, halo_recv
-    )
+    for copy in flag_copies:
+        copy.start()
+    halo = band_copies(control, above, below, halo_send, halo_recv, 6)
+    halo += side_copies(pack.at[0], pack.at[1], from_left, from_right, halo_send, halo_recv)
     for copy in halo:
         copy.start()
-
-    mine = owner_col == iota((n_slots, slots), 1) // BLOCK_COLS
+    for load in loads[4:]:
+        load.start()
+
+    lane_o = iota((1, slots), 1) // BLOCK_COLS
+    owner_o = lax.rem(choose(lane_o // n_row, rings) + far, n_far) * n_row + lane_o % n_row
+    mine = owner_col == owner_o
     cell = jnp.sum(jnp.where(mine, cells_col, 0), axis=0, keepdims=True)
     live = jnp.sum(mine.astype(F32), axis=0, keepdims=True)
     groups = width // BLOCK_COLS
@@ -272,7 +308,7 @@
         picks[rows, :] = pick * keep
         return carry
 
-    lax.fori_loop(0, height, lay, 0)
+    lax.fori_loop(0, height, lay, 0, unroll=True)
     rim = iota((side, slots), 0)
     for k, start in enumerate((-REACH, width)):
         value = jnp.where(rim // REACH == row_of, taps_at(rim % REACH + start), 0.0)
@@ -289,7 +325,7 @@
     band_high[...] = high
     band_low[...] = low
 
-    loads[1].wait()
+    loads[4].wait()
     for r in range(height):
         value = background[r]
         high, rest = split_two(value)
@@ -304,7 +340,8 @@
         gathered[:levels] + gathered[levels : 2 * levels] + gathered[2 * levels :]
     )
 
-    loads[2].wait()
+    for load in loads[5:7]:
+        load.wait()
     n_recv = radiance.shape[0] // BLOCK_COLS
     channels = radiance.shape[1]
     counts = jnp.sum(
@@ -321,29 +358,39 @@
         iota((n_recv * BLOCK_COLS, channels), 1) < counts, radiance[...].astype(F32), UNSEEN
     ).astype(BF16)
 
-    each(lambda d: flag_copy(d).wait_recv())
+    for copy in flag_copies:
+        copy.wait_recv()
     table = flags[...].reshape(n_lat, 128)
     sent = jnp.sum(
         jnp.where(iota((n_lat, 128), 1) == me, table, 0.0), axis=1, keepdims=True
     )
     sent = jnp.broadcast_to(sent, (n_lat, n_recv * BLOCK_COLS)).astype(BF16)
-    source = iota((slots, n_lat), 0) // BLOCK_COLS
-    entry = iota((slots, n_lat), 1)
-    present = dot((entry == source).astype(BF16), sent)
-    arrival = dot((entry < source).astype(BF16), sent)
-    slot_x = iota((slots, n_recv * BLOCK_COLS), 1)
-    row_x = iota((slots, n_recv * BLOCK_COLS), 0)
-    select = (
-        (present > 0.5)
-        & (arrival == (slot_x // BLOCK_COLS).astype(F32))
-        & (slot_x % BLOCK_COLS == row_x % BLOCK_COLS)
-    )
-    outgoing[...] = (
-        dot(select.astype(BF16), seen).reshape(n_lat, BLOCK_COLS, channels).astype(BF16)
-    )
-    own = pltpu.make_async_copy(outgoing.at[me], observed.at[me], local_sem.at[6])
+    half = slots // 2
+    rads = {}
+    for part in range(2):
+        row_o = (iota((half, n_lat), 0) + part * half) // BLOCK_COLS
+        source = lax.rem(choose(row_o // n_row, rings[::-1]) + far, n_far) * n_row + row_o % n_row
+        entry = iota((half, n_lat), 1)
+        present = dot((entry == source).astype(BF16), sent)
+        arrival = dot((entry < source).astype(BF16), sent)
+        slot_x = iota((half, n_recv * BLOCK_COLS), 1)
+        row_x = iota((half, n_recv * BLOCK_COLS), 0)
+        select = (
+            (present > 0.5)
+            & (arrival == (slot_x // BLOCK_COLS).astype(F32))
+            & (slot_x % BLOCK_COLS == row_x % BLOCK_COLS)
+        )
+        outgoing[pl.ds(part * (n_lat // 2), n_lat // 2)] = (
+            dot(select.astype(BF16), seen).reshape(n_lat // 2, BLOCK_COLS, channels).astype(BF16)
+        )
+        for df, dn in reaches:
+            if rings[::-1].index(df) * 2 // n_far == part:
+                rads[df, dn] = rad_copy(df, dn)
+                rads[df, dn].start()
+    own = pltpu.make_async_copy(
+        outgoing.at[(n_far - 1) * n_row + near], observed.at[near], local_sem.at[len(loads)]
+    )
     own.start()
-    each(lambda d: rad_copy(d).start())
 
     keep_above = jnp.where(me > 0, 1.0, 0.0).astype(F32)
     keep_below = jnp.where(me < n_lat - 1, 1.0, 0.0).astype(F32)
@@ -386,7 +433,7 @@
     )
     slot_rows[...] = profile.T.astype(BF16)
 
-    for load in loads[3:]:
+    for load in loads[7:]:
         load.wait()
     tile = 256
     hidden = w2.shape[0]
@@ -404,50 +451,99 @@
         act_two[:, at] = jnp.tanh(dot(act_one[...], w2[:, at]) + b2_ref[:, at]).astype(BF16)
         return carry
 
-    lax.fori_loop(0, hidden // tile, first, 0)
-    lax.fori_loop(0, hidden // tile, second, 0)
+    lax.fori_loop(0, hidden // tile, first, 0, unroll=True)
+    lax.fori_loop(0, hidden // tile, second, 0, unroll=True)
     emitted[...] = dot(act_two[...], w3[...]) + b3_ref[...]
 
     own.wait()
-    each(lambda d: rad_copy(d).wait_recv())
-    target = observed[...].astype(F32).reshape(slots, channels)
-    misfit = jnp.where(target < 0.5 * UNSEEN, emitted[...] - target, 0.0).astype(BF16)
-
-    def second_back(n, carry):
-        at = lanes_of(n)
-        value = act_two[:, at].astype(F32)
-        grad_two[:, at] = (dot(misfit, w3[at, :], NT) * (1.0 - value * value)).astype(BF16)
+    for part in range(2):
+        for df, dn in reaches:
+            if rings.index((n_far - df) % n_far) * 2 // n_far == part:
+                rads[df, dn].wait_recv()
+        rows = pl.ds(part * half, half)
+        target = observed[pl.ds(part * (n_lat // 2), n_lat // 2)].astype(F32).reshape(half, channels)
+        misfit[...] = jnp.where(
+            target < 0.5 * UNSEEN, emitted[rows, :] - target, 0.0
+        ).astype(BF16)
+
+        def second_back(n, carry):
+            at = lanes_of(n)
+            value = act_two[rows, at].astype(F32)
+            grad_two[:, at] = (dot(misfit[...], w3[at, :], NT) * (1.0 - value * value)).astype(BF16)
+            return carry
+
+        def first_back(n, carry):
+            at = lanes_of(n)
+            value = act_one[rows, at].astype(F32)
+            grad_one[rows, at] = (
+                dot(grad_two[...], w2[at, :], NT) * (1.0 - value * value)
+            ).astype(BF16)
+            return carry
+
+        lax.fori_loop(0, hidden // tile, second_back, 0, unroll=True)
+        lax.fori_loop(0, hidden // tile, first_back, 0, unroll=True)
+    sensitivity = dot(w1[...], grad_one[...], NT).astype(BF16)
+
+    edges = dot(sensitivity, taps_high[pl.ds(main, 2 * side), :], NT).astype(BF16)
+    for k in range(2):
+        rim_send[k] = edges[:, k * side : (k + 1) * side]
+    sides = side_copies(
+        rim_send.at[0], rim_send.at[1], left_back, right_back, back_send, back_recv
+    )
+    for copy in sides:
+        copy.start()
+    bands = []
+    chunk = height // CHUNKS
+    for part in range(CHUNKS):
+        rows = pl.ds(part * chunk, chunk)
+        spreadout = dot(sensitivity, taps_high[pl.ds(part * chunk * width, chunk * width), :], NT)
+        for r in range(chunk):
+            value = spreadout[:, r * width : (r + 1) * width]
+            landed[part * chunk + r] = value
+            landed_send[part * chunk + r] = value.astype(BF16)
+        bands += band_copies(
+            landed_send.at[rows], above_back.at[rows], below_back.at[rows],
+            back_send, back_recv, 6 + 2 * part,
+        )
+        for copy in bands[-2:]:
+            copy.start()
+
+    def own_rows(t, carry):
+        at = pl.ds(pl.multiple_of(t * 8, 8), 8)
+        values = [landed[r, at, :] for r in range(height)]
+        for r in range(height):
+            total = values[r] * LAT_TAPS[REACH]
+            for j in range(1, height):
+                pair = [values[k] for k in (r - j, r + j) if 0 <= k < height]
+                if pair:
+                    total += sum(pair[1:], pair[0]) * LAT_TAPS[REACH + j]
+            smooth[r, at, :] = total
         return carry
 
-    def first_back(n, carry):
-        at = lanes_of(n)
-        value = act_one[:, at].astype(F32)
-        grad_one[:, at] = (dot(grad_two[...], w2[at, :], NT) * (1.0 - value * value)).astype(BF16)
+    lax.fori_loop(0, levels // 8, own_rows, 0, unroll=True)
+    for copy in bands:
+        copy.wait_recv()
+    for r in range(height):
+        above[r] = above_back[r].astype(F32) * keep_above
+        below[r] = below_back[r].astype(F32) * keep_below
+
+    def other_rows(t, carry):
+        at = pl.ds(pl.multiple_of(t * 8, 8), 8)
+        upper = [above[r, at, :] for r in range(height)]
+        lower = [below[r, at, :] for r in range(height)]
+        for r in range(height):
+            total = smooth[r, at, :]
+            for k in range(height):
+                if r + height - k <= REACH:
+                    total += upper[k] * LAT_TAPS[REACH + r + height - k]
+                if k + height - r <= REACH:
+                    total += lower[k] * LAT_TAPS[REACH + k + height - r]
+            smooth[r, at, :] = total
         return carry
 
-    lax.fori_loop(0, hidden // tile, second_back, 0)
-    lax.fori_loop(0, hidden // tile, first_back, 0)
-    sensitivity = dot(w1[...], grad_one[...], NT).astype(BF16)
-
-    spreadout = dot(sensitivity, taps_high[...], NT)
-    for r in range(height):
-        value = spreadout[:, r * width : (r + 1) * width]
-        landed[r] = value
-        landed_send[r] = value.astype(BF16)
-    for k in range(2):
-        rim_send[k] = spreadout[:, main + k * side : main + (k + 1) * side].astype(BF16)
-    back = rim_copies(
-        landed_send, above_back, below_back, rim_send.at[0], rim_send.at[1],
-        left_back, right_back, back_send, back_recv,
-    )
-    for copy in back:
-        copy.start()
-    for copy in back:
+    lax.fori_loop(0, levels // 8, other_rows, 0, unroll=True)
+    for copy in sides:
         copy.wait_recv()
-
-    for r in range(height):
-        above[r] = above_back[r].astype(F32)
-        below[r] = below_back[r].astype(F32)
     for k, ref in enumerate((left_back, right_back)):
         for b in range(3):
             rims[pl.ds(k * levels, levels), pl.ds(b * side, side)] = (
@@ -456,25 +552,16 @@
     crossed = dot(rims[pl.ds(0, 2 * levels), :], band_high[...])
     for r in range(height):
         at = slice(r // per * width, (r // per + 1) * width)
-        value = control[r]
         low_cols = crossed[:levels, at]
         high_cols = crossed[levels:, at]
         shift = (-(r % per) * REACH) % width
         low_cols = pltpu.roll(low_cols, shift, 1) if shift else low_cols
         shift = (width - REACH - (r % per) * REACH) % width
         high_cols = pltpu.roll(high_cols, shift, 1) if shift else high_cols
-        value += jnp.where(lane < REACH, low_cols, 0.0)
-        value += jnp.where(lane >= width - REACH, high_cols, 0.0)
-        smooth[r] = value
-
-    def finish(r, at, value):
-        out_ref[r, at, :] = smooth[r, at, :] + value
-
-    smooth_rows(above, landed, below, keep_above, keep_below, height, levels, finish)
-
-    each(lambda d: flag_copy(d).wait_send())
-    each(lambda d: rad_copy(d).wait_send())
-    for copy in halo + back:
+        edge = jnp.where(lane < REACH, low_cols, jnp.where(lane >= width - REACH, high_cols, 0.0))
+        out_ref[r] = smooth[r] + edge
+
+    for copy in flag_copies + list(rads.values()) + halo + sides + bands:
         copy.wait_send()
 
 
@@ -504,19 +591,22 @@
     per_side = side // width
     dma = pltpu.SemaphoreType.DMA
     vmem = pltpu.VMEM
-    any_spec = pl.BlockSpec(memory_space=pl.ANY)
+    hbm_spec = pl.BlockSpec(memory_space=pltpu.HBM)
     vmem_spec = pl.BlockSpec(memory_space=pltpu.VMEM)
-    smem_spec = pl.BlockSpec(memory_space=pltpu.SMEM)
     grid = (height, levels, width)
-    return pl.pallas_call(
+    adjoint = pl.pallas_call(
         functools.partial(kernel, n_lat, n_lon),
         out_shape=jax.ShapeDtypeStruct(grid, F32),
-        in_specs=[
-            any_spec, any_spec, smem_spec, vmem_spec, vmem_spec, vmem_spec, any_spec,
-            any_spec, vmem_spec, any_spec, vmem_spec, any_spec, vmem_spec,
-        ],
+        in_specs=[hbm_spec] * 13,
         out_specs=vmem_spec,
         scratch_shapes=[
+            pltpu.SMEM(lon_width.shape, I32),
+            vmem((1, block_cells.shape[0]), I32),
+            vmem((1, block_owner.shape[0]), I32),
+            vmem((1, channel_count.shape[0]), I32),
+            vmem((1, hidden), F32),
+            vmem((1, hidden), F32),
+            vmem((1, channels), F32),
             vmem(grid, F32),
             vmem(grid, F32),
             vmem((recv_cols, channels), BF16),
@@ -544,9 +634,10 @@
             vmem((slots, levels), BF16),
             vmem((slots, hidden), BF16),
             vmem((slots, hidden), BF16),
-            vmem((slots, hidden), BF16),
+            vmem((slots // 2, hidden), BF16),
             vmem((slots, hidden), BF16),
             vmem((slots, channels), F32),
+            vmem((slots // 2, channels), BF16),
             vmem(grid, F32),
             vmem(grid, BF16),
             vmem((2, levels, side), BF16),
@@ -554,34 +645,40 @@
             vmem(grid, BF16),
             vmem((3, levels, side), BF16),
             vmem((3, levels, side), BF16),
-            dma((8,)),
+            dma((14,)),
             dma((n_lat,)),
             dma((n_lat,)),
             dma((n_lat,)),
             dma((n_lat,)),
             dma((8,)),
             dma((8,)),
-            dma((8,)),
-            dma((8,)),
+            dma((6 + 2 * CHUNKS,)),
+            dma((6 + 2 * CHUNKS,)),
         ],
         compiler_params=pltpu.CompilerParams(
-            collective_id=0, has_side_effects=True, vmem_limit_bytes=60 * 1024 * 1024
+            collective_id=0, has_side_effects=True, vmem_limit_bytes=26 * 1024 * 1024
         ),
     )(
-        control,
-        background,
-        lon_width,
-        block_cells.T,
-        block_owner.T,
-        channel_count.T,
-        radiance.T,
-        in_weight,
-        in_bias.reshape(1, -1),
-        mid_weight,
-        mid_bias.reshape(1, -1),
-        out_weight,
-        out_bias.reshape(1, -1),
-    )
+        *(
+            pltpu.with_memory_space_constraint(value, pltpu.HBM)
+            for value in (
+                control,
+                background,
+                lon_width,
+                block_cells.T,
+                block_owner.T,
+                channel_count.T,
+                radiance.T,
+                in_weight,
+                in_bias.reshape(1, -1),
+                mid_weight,
+                mid_bias.reshape(1, -1),
+                out_weight,
+                out_bias.reshape(1, -1),
+            )
+        )
+    )
+    return control + adjoint
 
 
 def solution(mesh):

time: 53.7 us -> 46.7 us (0.87)
  Pallas kernels: 51.6 us -> 45.8 us
  local copies, waits for them, and re-layouts: 1.67 us -> 0.01 us
  other arithmetic: 0 us -> 0.74 us
    pallas_call x1, Pallas kernels: 51.6 us -> 45.8 us  [shards(): pl.pallas_call(functools.partial(kernel, n_lat, n_lon), out_shape=jax.Sha...]
    unnamed x1 -> x2, local copies, waits for them, and re-layouts: 1.67 us -> 0.01 us
    add x0 -> x1, other arithmetic: none -> 0.74 us  [shards(): return control + adjoint]
where the time goes in v2:
time: 46.7 us; the launch traced here: 46.5 us
  Pallas kernels  45.8 us (98%)
  other arithmetic  0.74 us (2%)
    pallas_call x1, Pallas kernels, shards(): pl.pallas_call(functools.partial(kernel, n_lat, n_lon), out_shape=jax.Sha...  45.8 us

profile of v2, /device:TPU:1, one launch (start us, length us, event | category | flops | bytes accessed | tf_op | source)
XLA Modules:
  0.0 46.5 jit_solution(8736386780743145599)
XLA Ops:
  0.0 0.0 copy-start
  0.0 45.8 %shard_map.127 = f32[16,32,128]{2,1,0:T(8,128)S(1)} custom-call(f32[16,32,128]{2,1,0:T(8,128)} %control_hbm.1, f32[16,32,128]{2,1,0:T(8,128)} %background_hbm.1, s32[16]{0:T(128)} %width_hbm.1, s32[1,64]{1,0:T(1,128)} %bitcast.11, s32[1,64]{1,0:T(1,128)} %bitcast.12, s32[1,33]{1,0:T(1,128)} %bitcast.13, bf16[264,256]{1,0:T(8,128)(2,1)} %bitcast.7, ...), custom_call_target="tpu_custom_call" | custom-call | tf_op jit(solution)/shard_map/pallas_call | solution.py:597
  45.8 0.0 copy-done
  45.8 0.7 %add.3 = f32[16,32,128]{2,1,0:T(8,128)} add(f32[16,32,128]{2,1,0:T(8,128)S(1)} %copy-done, f32[16,32,128]{2,1,0:T(8,128)S(1)} %shard_map.127) | non-fusion elementwise | flops 65536 | bytes 786432 | tf_op jit(solution)/shard_map/add | solution.py:681
Async XLA Ops:
  0.0 45.8 %copy-start = (f32[16,32,128]{2,1,0:T(8,128)S(1)}, f32[16,32,128]{2,1,0:T(8,128)}, u32[]{:S(2)}) copy-start(f32[16,32,128]{2,1,0:T(8,128)} %control_hbm.1) | copy-start | bytes 786436

commit v3 on v2

--- a/solution.py
+++ b/solution.py
@@ -12,6 +12,8 @@
 BLOCK_COLS = 8
 LAT_SIGMA = 8.0
 CHUNKS = 4
+SEND_PARTS = 2
+BACK_PARTS = 1
 UNSEEN = 32768.0
 MESH = pl.DeviceIdType.MESH
 F32 = jnp.float32
@@ -121,6 +123,9 @@
     grad_one,
     emitted,
     misfit,
+    w2_turned,
+    w3_turned,
+    taps_turned,
     landed,
     landed_send,
     rim_send,
@@ -152,7 +157,10 @@
     far = me // n_row
     near = me - far * n_row
     rings = by_distance(n_far)
+    send_parts = min(SEND_PARTS, n_far)
+    back_parts = min(BACK_PARTS, n_far)
     reaches = [(df, dn) for df in rings[::-1] for dn in range(n_row) if df or dn]
+    reaches.sort(key=lambda d: -min(d[0], n_far - d[0]) - min(d[1], n_row - d[1]) / 2)
 
     def peer(df, dn):
         return lax.rem(far + df, n_far) * n_row + lax.rem(near + dn, n_row)
@@ -365,26 +373,26 @@
         jnp.where(iota((n_lat, 128), 1) == me, table, 0.0), axis=1, keepdims=True
     )
     sent = jnp.broadcast_to(sent, (n_lat, n_recv * BLOCK_COLS)).astype(BF16)
-    half = slots // 2
+    piece = slots // send_parts
     rads = {}
-    for part in range(2):
-        row_o = (iota((half, n_lat), 0) + part * half) // BLOCK_COLS
+    for part in range(send_parts):
+        row_o = (iota((piece, n_lat), 0) + part * piece) // BLOCK_COLS
         source = lax.rem(choose(row_o // n_row, rings[::-1]) + far, n_far) * n_row + row_o % n_row
-        entry = iota((half, n_lat), 1)
+        entry = iota((piece, n_lat), 1)
         present = dot((entry == source).astype(BF16), sent)
         arrival = dot((entry < source).astype(BF16), sent)
-        slot_x = iota((half, n_recv * BLOCK_COLS), 1)
-        row_x = iota((half, n_recv * BLOCK_COLS), 0)
+        slot_x = iota((piece, n_recv * BLOCK_COLS), 1)
+        row_x = iota((piece, n_recv * BLOCK_COLS), 0)
         select = (
             (present > 0.5)
             & (arrival == (slot_x // BLOCK_COLS).astype(F32))
             & (slot_x % BLOCK_COLS == row_x % BLOCK_COLS)
         )
-        outgoing[pl.ds(part * (n_lat // 2), n_lat // 2)] = (
-            dot(select.astype(BF16), seen).reshape(n_lat // 2, BLOCK_COLS, channels).astype(BF16)
+        outgoing[pl.ds(part * (n_lat // send_parts), n_lat // send_parts)] = (
+            dot(select.astype(BF16), seen).reshape(n_lat // send_parts, BLOCK_COLS, channels).astype(BF16)
         )
         for df, dn in reaches:
-            if rings[::-1].index(df) * 2 // n_far == part:
+            if rings[::-1].index(df) * send_parts // n_far == part:
                 rads[df, dn] = rad_copy(df, dn)
                 rads[df, dn].start()
     own = pltpu.make_async_copy(
@@ -455,13 +463,18 @@
     lax.fori_loop(0, hidden // tile, second, 0, unroll=True)
     emitted[...] = dot(act_two[...], w3[...]) + b3_ref[...]
 
+    w2_turned[...] = w2[...].T
+    w3_turned[...] = w3[...].T
+    taps_turned[...] = taps_high[...].T
+
     own.wait()
-    for part in range(2):
+    piece = slots // back_parts
+    for part in range(back_parts):
         for df, dn in reaches:
-            if rings.index((n_far - df) % n_far) * 2 // n_far == part:
+            if rings.index((n_far - df) % n_far) * back_parts // n_far == part:
                 rads[df, dn].wait_recv()
-        rows = pl.ds(part * half, half)
-        target = observed[pl.ds(part * (n_lat // 2), n_lat // 2)].astype(F32).reshape(half, channels)
+        rows = pl.ds(part * piece, piece)
+        target = observed[pl.ds(part * (n_lat // back_parts), n_lat // back_parts)].astype(F32).reshape(piece, channels)
         misfit[...] = jnp.where(
             target < 0.5 * UNSEEN, emitted[rows, :] - target, 0.0
         ).astype(BF16)
@@ -469,14 +482,14 @@
         def second_back(n, carry):
             at = lanes_of(n)
             value = act_two[rows, at].astype(F32)
-            grad_two[:, at] = (dot(misfit[...], w3[at, :], NT) * (1.0 - value * value)).astype(BF16)
+            grad_two[:, at] = (dot(misfit[...], w3_turned[:, at]) * (1.0 - value * value)).astype(BF16)
             return carry
 
         def first_back(n, carry):
             at = lanes_of(n)
             value = act_one[rows, at].astype(F32)
             grad_one[rows, at] = (
-                dot(grad_two[...], w2[at, :], NT) * (1.0 - value * value)
+                dot(grad_two[...], w2_turned[:, at]) * (1.0 - value * value)
             ).astype(BF16)
             return carry
 
@@ -484,7 +497,7 @@
         lax.fori_loop(0, hidden // tile, first_back, 0, unroll=True)
     sensitivity = dot(w1[...], grad_one[...], NT).astype(BF16)
 
-    edges = dot(sensitivity, taps_high[pl.ds(main, 2 * side), :], NT).astype(BF16)
+    edges = dot(sensitivity, taps_turned[:, pl.ds(main, 2 * side)]).astype(BF16)
     for k in range(2):
         rim_send[k] = edges[:, k * side : (k + 1) * side]
     sides = side_copies(
@@ -496,7 +509,7 @@
     chunk = height // CHUNKS
     for part in range(CHUNKS):
         rows = pl.ds(part * chunk, chunk)
-        spreadout = dot(sensitivity, taps_high[pl.ds(part * chunk * width, chunk * width), :], NT)
+        spreadout = dot(sensitivity, taps_turned[:, pl.ds(part * chunk * width, chunk * width)])
         for r in range(chunk):
             value = spreadout[:, r * width : (r + 1) * width]
             landed[part * chunk + r] = value
@@ -521,6 +534,8 @@
         return carry
 
     lax.fori_loop(0, levels // 8, own_rows, 0, unroll=True)
+    for copy in flag_copies + list(rads.values()) + halo:
+        copy.wait_send()
     for copy in bands:
         copy.wait_recv()
     for r in range(height):
@@ -561,7 +576,7 @@
         edge = jnp.where(lane < REACH, low_cols, jnp.where(lane >= width - REACH, high_cols, 0.0))
         out_ref[r] = smooth[r] + edge
 
-    for copy in flag_copies + list(rads.values()) + halo + sides + bands:
+    for copy in sides + bands:
         copy.wait_send()
 
 
@@ -586,6 +601,7 @@
     hidden = mid_weight.shape[0]
     channels, recv_cols = radiance.shape
     slots = n_lat * BLOCK_COLS
+    n_far = n_lat // (8 if n_lat % 16 == 0 else 2)
     main = height * width
     side = height * REACH
     per_side = side // width
@@ -634,10 +650,13 @@
             vmem((slots, levels), BF16),
             vmem((slots, hidden), BF16),
             vmem((slots, hidden), BF16),
-            vmem((slots // 2, hidden), BF16),
+            vmem((slots // min(BACK_PARTS, n_far), hidden), BF16),
             vmem((slots, hidden), BF16),
             vmem((slots, channels), F32),
-            vmem((slots // 2, channels), BF16),
+            vmem((slots // min(BACK_PARTS, n_far), channels), BF16),
+            vmem((hidden, hidden), BF16),
+            vmem((channels, hidden), BF16),
+            vmem((slots, main + 2 * side), BF16),
             vmem(grid, F32),
             vmem(grid, BF16),
             vmem((2, levels, side), BF16),
@@ -656,7 +675,7 @@
             dma((6 + 2 * CHUNKS,)),
         ],
         compiler_params=pltpu.CompilerParams(
-            collective_id=0, has_side_effects=True, vmem_limit_bytes=26 * 1024 * 1024
+            collective_id=0, has_side_effects=True, vmem_limit_bytes=36 * 1024 * 1024
         ),
     )(
         *(

time: 46.7 us -> 45.9 us (0.983)
  Pallas kernels: 45.8 us -> 45 us
    pallas_call x1, Pallas kernels: 45.8 us -> 45 us  [shards(): pl.pallas_call(functools.partial(kernel, n_lat, n_lon), out_shape=jax.Sha...]
where the time goes in v3:
time: 45.9 us; the launch traced here: 45.8 us
  Pallas kernels  45 us (98%)
  other arithmetic  0.74 us (2%)
    pallas_call x1, Pallas kernels, shards(): pl.pallas_call(functools.partial(kernel, n_lat, n_lon), out_shape=jax.Sha...  45 us

profile of v3, /device:TPU:1, one launch (start us, length us, event | category | flops | bytes accessed | tf_op | source)
XLA Modules:
  0.0 45.8 jit_solution(14296874370927336691)
XLA Ops:
  0.0 0.0 copy-start
  0.0 45.0 %shard_map.127 = f32[16,32,128]{2,1,0:T(8,128)S(1)} custom-call(f32[16,32,128]{2,1,0:T(8,128)} %control_hbm.1, f32[16,32,128]{2,1,0:T(8,128)} %background_hbm.1, s32[16]{0:T(128)} %width_hbm.1, s32[1,64]{1,0:T(1,128)} %bitcast.11, s32[1,64]{1,0:T(1,128)} %bitcast.12, s32[1,33]{1,0:T(1,128)} %bitcast.13, bf16[264,256]{1,0:T(8,128)(2,1)} %bitcast.7, ...), custom_call_target="tpu_custom_call" | custom-call | tf_op jit(solution)/shard_map/pallas_call | solution.py:613
  45.0 0.0 copy-done
  45.0 0.7 %add.3 = f32[16,32,128]{2,1,0:T(8,128)} add(f32[16,32,128]{2,1,0:T(8,128)S(1)} %copy-done, f32[16,32,128]{2,1,0:T(8,128)S(1)} %shard_map.127) | non-fusion elementwise | flops 65536 | bytes 786432 | tf_op jit(solution)/shard_map/add | solution.py:700
Async XLA Ops:
  0.0 45.0 %copy-start = (f32[16,32,128]{2,1,0:T(8,128)S(1)}, f32[16,32,128]{2,1,0:T(8,128)}, u32[]{:S(2)}) copy-start(f32[16,32,128]{2,1,0:T(8,128)} %control_hbm.1) | copy-start | bytes 786436

commit v4 on v3

--- a/solution.py
+++ b/solution.py
@@ -123,6 +123,7 @@
     grad_one,
     emitted,
     misfit,
+    w1_turned,
     w2_turned,
     w3_turned,
     taps_turned,
@@ -211,24 +212,11 @@
         (owner_col == iota((n_slots, 128), 1)).astype(F32), axis=0, keepdims=True
     ).reshape(1, 1, 128)
 
-    loads[3].wait()
-    lane = iota((levels, width), 1)
-    per = width // REACH
-    for k, start in enumerate((0, width - REACH)):
-        for group in range(height // per):
-            packed = jnp.zeros((levels, width), F32)
-            for r in range(per):
-                shift = (r * REACH - start) % width
-                value = control[group * per + r]
-                value = pltpu.roll(value, shift, 1) if shift else value
-                packed = jnp.where(lane // REACH == r, value, packed)
-            pack[k, group] = packed
-
     pl.semaphore_wait(barrier, n_lat - 1 + 6)
 
     def side_copies(left_src, right_src, left_dst, right_dst, send, recv):
         copies = []
-        for dl in (-1, 0, 1):
+        for dl in (-1, 1, 0):
             k = dl + 1
             copies.append(
                 pltpu.make_async_remote_copy(
@@ -272,6 +260,19 @@
 
     for copy in flag_copies:
         copy.start()
+    loads[3].wait()
+    lane = iota((levels, width), 1)
+    per = width // REACH
+    for k, start in enumerate((0, width - REACH)):
+        for group in range(height // per):
+            packed = jnp.zeros((levels, width), F32)
+            for r in range(per):
+                shift = (r * REACH - start) % width
+                value = control[group * per + r]
+                value = pltpu.roll(value, shift, 1) if shift else value
+                packed = jnp.where(lane // REACH == r, value, packed)
+            pack[k, group] = packed
+
     halo = band_copies(control, above, below, halo_send, halo_recv, 6)
     halo += side_copies(pack.at[0], pack.at[1], from_left, from_right, halo_send, halo_recv)
     for copy in halo:
@@ -463,6 +464,7 @@
     lax.fori_loop(0, hidden // tile, second, 0, unroll=True)
     emitted[...] = dot(act_two[...], w3[...]) + b3_ref[...]
 
+    w1_turned[...] = w1[...].T
     w2_turned[...] = w2[...].T
     w3_turned[...] = w3[...].T
     taps_turned[...] = taps_high[...].T
@@ -495,7 +497,7 @@
 
         lax.fori_loop(0, hidden // tile, second_back, 0, unroll=True)
         lax.fori_loop(0, hidden // tile, first_back, 0, unroll=True)
-    sensitivity = dot(w1[...], grad_one[...], NT).astype(BF16)
+    sensitivity = dot(grad_one[...], w1_turned[...]).T.astype(BF16)
 
     edges = dot(sensitivity, taps_turned[:, pl.ds(main, 2 * side)]).astype(BF16)
     for k in range(2):
@@ -654,6 +656,7 @@
             vmem((slots, hidden), BF16),
             vmem((slots, channels), F32),
             vmem((slots // min(BACK_PARTS, n_far), channels), BF16),
+            vmem((hidden, levels), BF16),
             vmem((hidden, hidden), BF16),
             vmem((channels, hidden), BF16),
             vmem((slots, main + 2 * side), BF16),

time: 45.9 us -> 45.3 us (0.987)
  Pallas kernels: 45 us -> 44.4 us
    pallas_call x1, Pallas kernels: 45 us -> 44.4 us  [shards(): pl.pallas_call(functools.partial(kernel, n_lat, n_lon), out_shape=jax.Sha...]
where the time goes in v4:
time: 45.3 us; the launch traced here: 45.2 us
  Pallas kernels  44.4 us (98%)
  other arithmetic  0.74 us (2%)
    pallas_call x1, Pallas kernels, shards(): pl.pallas_call(functools.partial(kernel, n_lat, n_lon), out_shape=jax.Sha...  44.4 us

profile of v4, /device:TPU:1, one launch (start us, length us, event | category | flops | bytes accessed | tf_op | source)
XLA Modules:
  0.0 45.2 jit_solution(16030552972212670081)
XLA Ops:
  0.0 0.0 copy-start
  0.0 44.4 %shard_map.127 = f32[16,32,128]{2,1,0:T(8,128)S(1)} custom-call(f32[16,32,128]{2,1,0:T(8,128)} %control_hbm.1, f32[16,32,128]{2,1,0:T(8,128)} %background_hbm.1, s32[16]{0:T(128)} %width_hbm.1, s32[1,64]{1,0:T(1,128)} %bitcast.11, s32[1,64]{1,0:T(1,128)} %bitcast.12, s32[1,33]{1,0:T(1,128)} %bitcast.13, bf16[264,256]{1,0:T(8,128)(2,1)} %bitcast.7, ...), custom_call_target="tpu_custom_call" | custom-call | tf_op jit(solution)/shard_map/pallas_call | solution.py:615
  44.4 0.0 copy-done
  44.4 0.7 %add.3 = f32[16,32,128]{2,1,0:T(8,128)} add(f32[16,32,128]{2,1,0:T(8,128)S(1)} %copy-done, f32[16,32,128]{2,1,0:T(8,128)S(1)} %shard_map.127) | non-fusion elementwise | flops 65536 | bytes 786432 | tf_op jit(solution)/shard_map/add | solution.py:703
Async XLA Ops:
  0.0 44.4 %copy-start = (f32[16,32,128]{2,1,0:T(8,128)S(1)}, f32[16,32,128]{2,1,0:T(8,128)}, u32[]{:S(2)}) copy-start(f32[16,32,128]{2,1,0:T(8,128)} %control_hbm.1) | copy-start | bytes 786436
